TPU v7x, 32 devices: a whole 2x2x4 slice. The times are simulated.
32 devices in a mesh: gx: 4 (over z), gy: 8 (over y, x, core).
Axes of the slice: x: 2, y: 2, z: 4, core: 2. Of those that a mesh axis runs over, the one named last changes fastest.
Arguments:
- displacement: float32 [3, 128, 5, 1024], P(None, 'gx', None, 'gy'), may hold values from -5 to 5
- velocity: float32 [3, 128, 5, 1024], P(None, 'gx', None, 'gy'), may hold values from -4 to 4
- stiffness: float32 [128, 5, 1024], P('gx', None, 'gy'), may hold values from 0.5 to 2
- inverse_mass: float32 [128, 5, 1024], P('gx', None, 'gy'), may hold values from 0.5 to 2
- facing: int32 [128, 8, 8], P('gx', 'gy'), may hold values from 0 to 1023, as said below
Outputs:
- final_displacement: float32 [3, 128, 5, 1024], P(None, 'gx', None, 'gy')
- final_velocity: float32 [3, 128, 5, 1024], P(None, 'gx', None, 'gy')
Inputs may be any that keep to these rules, and one draw needn't show every extreme that they name: facing[x, j, k] names block x' * 8 + j'. For each aligned run of 32 rows x and each j, the 256 entries name blocks with each pair (x' // 32, j') exactly 8 times; repeats are allowed.
All inputs are finite; a program needn't handle non-finite values.
Results may differ from a plain program's by a relative error of at most 0.0001.
Values sent between devices are 32-bit elements; how exact they have to be, the bound alone decides.
A program may use at most 64 MiB of HBM per device.

v0:
```python
import jax
import jax.numpy as jnp
from jax import lax
from jax.sharding import PartitionSpec as P

STEPS = 2


time_step = 0.2
penalty = 4.0
damping = 1.0
kernel_width = 4.0
frame_extent = 4.0


def with_halo(cells, sides, width):
    for axis, dim in sides:
        count = lax.axis_size(axis)
        ends = count - 1
        head = lax.slice_in_dim(cells, 0, width, axis=dim)
        tail = lax.slice_in_dim(cells, cells.shape[dim] - width, cells.shape[dim], axis=dim)
        cells = jnp.concatenate(
            [
                lax.ppermute(tail, axis, [(i, (i + 1) % count) for i in range(ends)]),
                cells,
                lax.ppermute(head, axis, [((i + 1) % count, i) for i in range(ends)]),
            ],
            axis=dim,
        )
    return cells


def block_frame(block_size):
    place = (jnp.arange(block_size, dtype=jnp.float32) - (block_size - 1) / 2.0) * (
        frame_extent / block_size
    )
    zero_row = jnp.zeros((block_size,), jnp.float32)
    return jnp.stack([zero_row, place, zero_row], axis=0)


def pair_forces(own_block, facing_blocks):
    block_size = own_block.shape[-1]
    frame = block_frame(block_size)
    own_disp = own_block[:, :3] + frame
    own_vel = own_block[:, 3:]
    far_disp = facing_blocks[:, :, :3] + frame
    far_vel = facing_blocks[:, :, 3:]
    gaps = own_disp[:, None, :, :, None] - far_disp[:, :, :, None, :]
    spread = jnp.sum(gaps * gaps, axis=2)
    weights = jnp.exp(-spread / kernel_width)
    row_total = jnp.sum(weights, axis=3)
    col_total = jnp.sum(weights, axis=2)
    highest = lax.Precision.HIGHEST
    pulled_disp = jnp.einsum("gpij,gpcj->gpci", weights, far_disp, precision=highest)
    pulled_vel = jnp.einsum("gpij,gpcj->gpci", weights, far_vel, precision=highest)
    pushed_disp = jnp.einsum("gpij,gci->gpcj", weights, own_disp, precision=highest)
    pushed_vel = jnp.einsum("gpij,gci->gpcj", weights, own_vel, precision=highest)
    stiff_coef = penalty / (8.0 * block_size)
    damp_coef = damping / (8.0 * block_size)
    row_wide = row_total[:, :, None, :]
    col_wide = col_total[:, :, None, :]
    action = jnp.sum(
        stiff_coef * (own_disp[:, None] * row_wide - pulled_disp)
        + damp_coef * (pulled_vel - own_vel[:, None] * row_wide),
        axis=1,
    )
    reaction = -(
        stiff_coef * (pushed_disp - far_disp * col_wide)
        + damp_coef * (far_vel * col_wide - pushed_vel)
    )
    return (action, reaction)


def internal_force(padded_disp, padded_stiff, displacement):
    size_x, size_z, size_y = displacement.shape[1:]
    corner_sum = jnp.zeros((3, size_x + 1, size_z + 1, size_y + 1), jnp.float32)
    for shift_x in (0, 1):
        for shift_z in (0, 1):
            for shift_y in (0, 1):
                corner_sum = (
                    corner_sum
                    + padded_disp[
                        :,
                        shift_x : shift_x + size_x + 1,
                        shift_z : shift_z + size_z + 1,
                        shift_y : shift_y + size_y + 1,
                    ]
                )
    mean_disp = corner_sum / 8.0
    element_stiff = padded_stiff[: size_x + 1, : size_z + 1, : size_y + 1]
    weighted = element_stiff[None] * mean_disp
    node_stiff = jnp.zeros((size_x, size_z, size_y), jnp.float32)
    node_pull = jnp.zeros((3, size_x, size_z, size_y), jnp.float32)
    for shift_x in (0, 1):
        for shift_z in (0, 1):
            for shift_y in (0, 1):
                node_stiff = (
                    node_stiff
                    + element_stiff[
                        shift_x : shift_x + size_x,
                        shift_z : shift_z + size_z,
                        shift_y : shift_y + size_y,
                    ]
                )
                node_pull = (
                    node_pull
                    + weighted[
                        :,
                        shift_x : shift_x + size_x,
                        shift_z : shift_z + size_z,
                        shift_y : shift_y + size_y,
                    ]
                )
    return node_pull - displacement * node_stiff


def deliver_answers(answers, count_gx, count_gy, capacity):
    shaped = answers.reshape((count_gx * count_gy, capacity) + answers.shape[1:])
    arrived = lax.all_to_all(shaped, ("gx", "gy"), split_axis=0, concat_axis=0, tiled=True)
    return arrived.reshape(answers.shape)


def deliver_reactions(outgoing, count_gx, count_gy, capacity):
    shaped = outgoing.reshape((count_gx * count_gy, capacity) + outgoing.shape[1:])
    arrived = lax.all_to_all(shaped, ("gx", "gy"), split_axis=0, concat_axis=0, tiled=True)
    return arrived.reshape(outgoing.shape)


def local(displacement, velocity, stiffness, inverse_mass, facing):
    count_gx = lax.axis_size("gx")
    count_gy = lax.axis_size("gy")
    devices_all = count_gx * count_gy
    width_x, depth, width_y = stiffness.shape
    global_x = lax.axis_index("gx") * width_x + jnp.arange(width_x, dtype=jnp.int32)
    global_y = lax.axis_index("gy") * width_y + jnp.arange(width_y, dtype=jnp.int32)
    layer_index = jnp.arange(depth, dtype=jnp.int32)
    inside = (
        (global_x < width_x * count_gx - 1)[:, None, None]
        & (layer_index < depth - 1)[None, :, None]
        & (global_y < width_y * count_gy - 1)[None, None, :]
    )
    masked_stiff = jnp.where(inside, stiffness, 0.0)
    requests = 8 * width_x
    capacity = requests // devices_all
    wanted_ids = facing.reshape(requests)
    wanted_x = wanted_ids // count_gy
    owner_device = wanted_x // width_x * count_gy + wanted_ids % count_gy
    local_row = wanted_x % width_x
    ordinal = jnp.arange(requests, dtype=jnp.int32)
    earlier = (owner_device[:, None] == owner_device[None, :]) & (
        ordinal[None, :] < ordinal[:, None]
    )
    position = owner_device * capacity + jnp.sum(earlier.astype(jnp.int32), axis=1)
    request_rows = jnp.zeros((requests,), jnp.int32).at[position].set(local_row)
    asked_rows = lax.all_to_all(
        request_rows.reshape(devices_all, capacity),
        ("gx", "gy"),
        split_axis=0,
        concat_axis=0,
        tiled=True,
    ).reshape(requests)
    home_table = (asked_rows[None, :] == jnp.arange(width_x, dtype=jnp.int32)[:, None]).astype(
        jnp.float32
    )
    group_size = 16
    group_count = width_x // group_size

    def visit_group(pair_data):
        return pair_forces(pair_data[0], pair_data[1])

    for repeat in range(STEPS):
        stacked = jnp.concatenate([displacement, masked_stiff[None]], axis=0)
        padded = with_halo(stacked, (("gx", 1), ("gy", 3)), 1)
        padded = jnp.pad(padded, ((0, 0), (0, 0), (1, 1), (0, 0)))
        internal = internal_force(padded[:3], padded[3], displacement)
        surface = jnp.concatenate(
            [displacement[:, :, depth - 1, :], velocity[:, :, depth - 1, :]], axis=0
        ).transpose(1, 0, 2)
        answers = surface[asked_rows]
        arrived = deliver_answers(answers, count_gx, count_gy, capacity)
        facing_blocks = arrived[position].reshape(group_count, group_size, 8, 6, width_y)
        action, reaction = lax.map(
            visit_group, (surface.reshape(group_count, group_size, 6, width_y), facing_blocks)
        )
        action = action.reshape(width_x, 3, width_y)
        outgoing = (
            jnp.zeros((requests, 3, width_y), jnp.float32)
            .at[position]
            .set(reaction.reshape(requests, 3, width_y))
        )
        returned = deliver_reactions(outgoing, count_gx, count_gy, capacity)
        home_part = jnp.einsum(
            "rq,qn->rn",
            home_table,
            returned.reshape(requests, 3 * width_y),
            precision=lax.Precision.HIGHEST,
        ).reshape(width_x, 3, width_y)
        contact = (action + home_part).transpose(1, 0, 2)
        total_force = internal.at[:, :, depth - 1, :].add(contact)
        velocity = velocity + time_step * inverse_mass[None] * total_force
        displacement = displacement + time_step * velocity
    return (displacement, velocity)


def solution(mesh):
    in_specs = (
        P(None, "gx", None, "gy"),
        P(None, "gx", None, "gy"),
        P("gx", None, "gy"),
        P("gx", None, "gy"),
        P("gx", "gy", None),
    )
    out_specs = (P(None, "gx", None, "gy"), P(None, "gx", None, "gy"))
    return jax.shard_map(local, mesh=mesh, in_specs=in_specs, out_specs=out_specs, check_vma=False)
```

profile of v0, /device:TPU:0, one launch (start us, length us, event | category | flops | bytes accessed | tf_op | source)
XLA Modules:
  0.0 410.1 jit_solution(13143281751323073011)
XLA Ops:
  4.0 7.3 %all-to-all-start = ((s32[32,1,8]{2,1,0:T(1,128)}), s32[32,1,8]{2,1,0:T(1,128)S(1)}, u32[]{:S(2)}, u32[]{:S(2)}) async-start(s32[32,1,8]{2,1,0:T(1,128)} %bitcast.28), calls=%async_computation | async-start | bytes 32768 | tf_op jit(solution)/shard_map/all_to_all | solution.py:155
  13.2 5.3 %all-to-all-done = s32[32,1,8]{2,1,0:T(1,128)S(1)} async-done(((s32[32,1,8]{2,1,0:T(1,128)}), s32[32,1,8]{2,1,0:T(1,128)S(1)}, u32[]{:S(2)}, u32[]{:S(2)}) %all-to-all-start) | async-done | bytes 1056 | tf_op jit(solution)/shard_map/all_to_all | solution.py:155
  50.2 115.4 %while.30 = (s32[]{:T(128)}, f32[2,16,3,128]{3,1,0,2:T(8,128)S(1)}, f32[2,16,8,3,128]{4,3,2,1,0:T(4,128)}, f32[2,16,6,128]{3,2,1,0:T(8,128)S(1)}, f32[2,16,8,6,128]{4,3,2,1,0:T(8,128)}, /*index=5*/s32[]{:T(128)}, f32[]{:T(128)}) while((s32[]{:T(128)}, f32[2,16,3,128]{3,1,0,2:T(8,128)S(1)}, f32[2,16,8,3,128]{4,3,2,1,0:T(4,128)}, ...), condition=%wide.region_7.8_spmd, body=%wide.region_2.7_spmd.sunk | while | flops 344736768 | bytes 54557288 | solution.py:182
  81.0 13.1 %fusion.103 = f32[16,8,3,128]{3,2,1,0:T(4,128)S(1)} fusion(f32[16,8,3,128]{3,2,1,0:T(4,128)S(1)} %slice_add_fusion.49, f32[16,8,128,128]{3,2,1,0:T(8,128)S(1)} %multiply_reduce_fusion.4, f32[16,8,128]{2,1,0:T(8,128)S(1)} %get-tuple-element.306, f32[16,3,128]{2,1,0:T(4,128)S(1)} %get-tuple-element.305), kind=kOutput, calls=%fused_computation.23.clone.1 | convolution fusion | flops 79839232 | bytes 8871936 | tf_op jit(solution)/shard_map/while/body/eval_jaxpr/gpij,gpcj->gpci/dot_general | solution.py:54
  94.1 13.2 %fusion.104 = f32[16,3,128]{2,1,0:T(4,128)S(1)} fusion(f32[16,8,3,128]{3,2,1,0:T(4,128)S(1)} %fusion.103, f32[16,8,128,128]{3,2,1,0:T(8,128)S(1)} %multiply_reduce_fusion.4, f32[16,8,6,128]{3,2,1,0:T(8,128)S(1)} %dynamic-slice_bitcast_fusion.6, f32[16,3,128]{2,1,0:T(4,128)S(1)} %get-tuple-element.307, f32[16,8,128]{2,1,0:T(8,128)S(1)} %get-tuple-element.306), kind=kOutput, calls=%fused_computation.24.clone.1 | convolution fusion | flops 79931392 | bytes 9035776 | tf_op jit(solution)/shard_map/while/body/eval_jaxpr/gpij,gpcj->gpci/dot_general | solution.py:55
  107.3 4.8 %fusion.105 = f32[16,8,3,128]{3,2,1,0:T(4,128)S(1)} fusion(f32[16,8,128,128]{3,2,1,0:T(8,128)S(1)} %multiply_reduce_fusion.4, f32[16,8,6,128]{3,2,1,0:T(8,128)S(1)} %dynamic-slice_bitcast_fusion.6, f32[16,8,128]{2,1,0:T(8,128)S(1)} %get-tuple-element.308, f32[16,6,128]{2,1,0:T(8,128)S(1)} %dynamic-slice_bitcast_fusion.7), kind=kOutput, calls=%fused_computation.11.clone.1 | convolution fusion | flops 79839232 | bytes 8945664 | tf_op jit(solution)/shard_map/while/body/eval_jaxpr/gpij,gci->gpcj/dot_general | solution.py:57
  112.1 5.5 %fusion.106 = f32[2,16,8,3,128]{4,3,2,1,0:T(4,128)} fusion(f32[2,16,8,3,128]{4,3,2,1,0:T(4,128)} %get-tuple-element.327, s32[]{:T(128)S(6)} %copy.135, f32[16,8,3,128]{3,2,1,0:T(4,128)S(1)} %fusion.105, f32[16,8,128,128]{3,2,1,0:T(8,128)S(1)} %multiply_reduce_fusion.4, f32[16,8,3,128]{3,2,1,0:T(4,128)S(1)} %slice_add_fusion.49, ...), kind=kOutput, calls=%fused_computation.18.clone.1 | convolution fusion | flops 79937536 | bytes 9134084 | tf_op jit(solution)/shard_map/while/body/eval_jaxpr/gpij,gci->gpcj/dot_general | solution.py:56
  124.8 13.1 %fusion.103 = f32[16,8,3,128]{3,2,1,0:T(4,128)S(1)} fusion(f32[16,8,3,128]{3,2,1,0:T(4,128)S(1)} %slice_add_fusion.49, f32[16,8,128,128]{3,2,1,0:T(8,128)S(1)} %multiply_reduce_fusion.4, f32[16,8,128]{2,1,0:T(8,128)S(1)} %get-tuple-element.306, f32[16,3,128]{2,1,0:T(4,128)S(1)} %get-tuple-element.305), kind=kOutput, calls=%fused_computation.23.clone.1 | convolution fusion | flops 79839232 | bytes 8871936 | tf_op jit(solution)/shard_map/while/body/eval_jaxpr/gpij,gpcj->gpci/dot_general | solution.py:54
  137.9 13.2 %fusion.104 = f32[16,3,128]{2,1,0:T(4,128)S(1)} fusion(f32[16,8,3,128]{3,2,1,0:T(4,128)S(1)} %fusion.103, f32[16,8,128,128]{3,2,1,0:T(8,128)S(1)} %multiply_reduce_fusion.4, f32[16,8,6,128]{3,2,1,0:T(8,128)S(1)} %dynamic-slice_bitcast_fusion.6, f32[16,3,128]{2,1,0:T(4,128)S(1)} %get-tuple-element.307, f32[16,8,128]{2,1,0:T(8,128)S(1)} %get-tuple-element.306), kind=kOutput, calls=%fused_computation.24.clone.1 | convolution fusion | flops 79931392 | bytes 9035776 | tf_op jit(solution)/shard_map/while/body/eval_jaxpr/gpij,gpcj->gpci/dot_general | solution.py:55
  151.1 4.8 %fusion.105 = f32[16,8,3,128]{3,2,1,0:T(4,128)S(1)} fusion(f32[16,8,128,128]{3,2,1,0:T(8,128)S(1)} %multiply_reduce_fusion.4, f32[16,8,6,128]{3,2,1,0:T(8,128)S(1)} %dynamic-slice_bitcast_fusion.6, f32[16,8,128]{2,1,0:T(8,128)S(1)} %get-tuple-element.308, f32[16,6,128]{2,1,0:T(8,128)S(1)} %dynamic-slice_bitcast_fusion.7), kind=kOutput, calls=%fused_computation.11.clone.1 | convolution fusion | flops 79839232 | bytes 8945664 | tf_op jit(solution)/shard_map/while/body/eval_jaxpr/gpij,gci->gpcj/dot_general | solution.py:57
  155.8 5.5 %fusion.106 = f32[2,16,8,3,128]{4,3,2,1,0:T(4,128)} fusion(f32[2,16,8,3,128]{4,3,2,1,0:T(4,128)} %get-tuple-element.327, s32[]{:T(128)S(6)} %copy.135, f32[16,8,3,128]{3,2,1,0:T(4,128)S(1)} %fusion.105, f32[16,8,128,128]{3,2,1,0:T(8,128)S(1)} %multiply_reduce_fusion.4, f32[16,8,3,128]{3,2,1,0:T(4,128)S(1)} %slice_add_fusion.49, ...), kind=kOutput, calls=%fused_computation.18.clone.1 | convolution fusion | flops 79937536 | bytes 9134084 | tf_op jit(solution)/shard_map/while/body/eval_jaxpr/gpij,gci->gpcj/dot_general | solution.py:56
  165.8 16.3 %scatter_fusion = f32[256,3,128]{2,1,0:T(4,128)S(1)} fusion(f32[256,3,128]{2,1,0:T(4,128)S(1)} %broadcast.537.clone, s32[256]{0:T(256)S(1)} %bitcast.217, f32[256,3,128]{2,1,0:T(4,128)} %bitcast.35), kind=kCustom, calls=%fused_computation.5 | custom fusion | bytes 1180672 | tf_op jit(solution)/shard_map/scatter | solution.py:189
  182.9 18.0 %all-to-all-start.2 = ((f32[32,8,3,128]{3,1,2,0:T(8,128)}), f32[32,8,3,128]{3,1,2,0:T(8,128)S(1)}, u32[]{:S(2)}, u32[]{:S(2)}) async-start(f32[32,8,3,128]{3,1,2,0:T(8,128)} %copy.77), calls=%async_computation.2 | async-start | bytes 786432 | tf_op jit(solution)/shard_map/all_to_all | solution.py:125
  204.8 9.3 %all-to-all-done.2 = f32[32,8,3,128]{3,1,2,0:T(8,128)S(1)} async-done(((f32[32,8,3,128]{3,1,2,0:T(8,128)}), f32[32,8,3,128]{3,1,2,0:T(8,128)S(1)}, u32[]{:S(2)}, u32[]{:S(2)}) %all-to-all-start.2) | async-done | bytes 393248 | tf_op jit(solution)/shard_map/all_to_all | solution.py:125
  244.4 115.2 %while.31 = (s32[]{:T(128)}, f32[2,16,3,128]{3,1,0,2:T(8,128)S(1)}, f32[2,16,8,3,128]{4,3,2,1,0:T(4,128)}, f32[2,16,6,128]{3,1,0,2:T(8,128)}, f32[2,16,8,6,128]{4,3,2,1,0:T(8,128)}, /*index=5*/s32[]{:T(128)}, f32[]{:T(128)}) while((s32[]{:T(128)}, f32[2,16,3,128]{3,1,0,2:T(8,128)S(1)}, f32[2,16,8,3,128]{4,3,2,1,0:T(4,128)}, ...), condition=%wide.region_14.15_spmd, body=%wide.region_9.14_spmd.sunk | while | flops 344736768 | bytes 54655592 | solution.py:182
  276.0 13.1 %fusion.113 = f32[16,8,3,128]{3,2,1,0:T(4,128)S(1)} fusion(f32[16,8,3,128]{3,2,1,0:T(4,128)S(1)} %slice_add_fusion.50, f32[16,8,128,128]{3,2,1,0:T(8,128)S(1)} %multiply_reduce_fusion.5, f32[16,8,128]{2,1,0:T(8,128)S(1)} %get-tuple-element.315, f32[16,3,128]{2,1,0:T(4,128)S(1)} %get-tuple-element.314), kind=kOutput, calls=%fused_computation.58.clone.1 | convolution fusion | flops 79839232 | bytes 8871936 | tf_op jit(solution)/shard_map/while/body/eval_jaxpr/gpij,gpcj->gpci/dot_general | solution.py:54
  289.1 13.2 %fusion.114 = f32[16,3,128]{2,1,0:T(4,128)S(1)} fusion(f32[16,8,3,128]{3,2,1,0:T(4,128)S(1)} %fusion.113, f32[16,8,128,128]{3,2,1,0:T(8,128)S(1)} %multiply_reduce_fusion.5, f32[16,8,6,128]{3,2,1,0:T(8,128)S(1)} %dynamic-slice_bitcast_fusion.8, f32[16,3,128]{2,1,0:T(4,128)S(1)} %get-tuple-element.316, f32[16,8,128]{2,1,0:T(8,128)S(1)} %get-tuple-element.315), kind=kOutput, calls=%fused_computation.59.clone.1 | convolution fusion | flops 79931392 | bytes 9035776 | tf_op jit(solution)/shard_map/while/body/eval_jaxpr/gpij,gpcj->gpci/dot_general | solution.py:55
  307.0 5.5 %fusion.116 = f32[2,16,8,3,128]{4,3,2,1,0:T(4,128)} fusion(f32[2,16,8,3,128]{4,3,2,1,0:T(4,128)} %get-tuple-element.348, s32[]{:T(128)S(6)} %copy.146, f32[16,8,3,128]{3,2,1,0:T(4,128)S(1)} %fusion.115, f32[16,8,128,128]{3,2,1,0:T(8,128)S(1)} %multiply_reduce_fusion.5, f32[16,8,3,128]{3,2,1,0:T(4,128)S(1)} %slice_add_fusion.50, ...), kind=kOutput, calls=%fused_computation.53.clone.1 | convolution fusion | flops 79937536 | bytes 9134084 | tf_op jit(solution)/shard_map/while/body/eval_jaxpr/gpij,gci->gpcj/dot_general | solution.py:56
  320.6 13.1 %fusion.113 = f32[16,8,3,128]{3,2,1,0:T(4,128)S(1)} fusion(f32[16,8,3,128]{3,2,1,0:T(4,128)S(1)} %slice_add_fusion.50, f32[16,8,128,128]{3,2,1,0:T(8,128)S(1)} %multiply_reduce_fusion.5, f32[16,8,128]{2,1,0:T(8,128)S(1)} %get-tuple-element.315, f32[16,3,128]{2,1,0:T(4,128)S(1)} %get-tuple-element.314), kind=kOutput, calls=%fused_computation.58.clone.1 | convolution fusion | flops 79839232 | bytes 8871936 | tf_op jit(solution)/shard_map/while/body/eval_jaxpr/gpij,gpcj->gpci/dot_general | solution.py:54
  333.7 13.2 %fusion.114 = f32[16,3,128]{2,1,0:T(4,128)S(1)} fusion(f32[16,8,3,128]{3,2,1,0:T(4,128)S(1)} %fusion.113, f32[16,8,128,128]{3,2,1,0:T(8,128)S(1)} %multiply_reduce_fusion.5, f32[16,8,6,128]{3,2,1,0:T(8,128)S(1)} %dynamic-slice_bitcast_fusion.8, f32[16,3,128]{2,1,0:T(4,128)S(1)} %get-tuple-element.316, f32[16,8,128]{2,1,0:T(8,128)S(1)} %get-tuple-element.315), kind=kOutput, calls=%fused_computation.59.clone.1 | convolution fusion | flops 79931392 | bytes 9035776 | tf_op jit(solution)/shard_map/while/body/eval_jaxpr/gpij,gpcj->gpci/dot_general | solution.py:55
  351.6 5.5 %fusion.116 = f32[2,16,8,3,128]{4,3,2,1,0:T(4,128)} fusion(f32[2,16,8,3,128]{4,3,2,1,0:T(4,128)} %get-tuple-element.348, s32[]{:T(128)S(6)} %copy.146, f32[16,8,3,128]{3,2,1,0:T(4,128)S(1)} %fusion.115, f32[16,8,128,128]{3,2,1,0:T(8,128)S(1)} %multiply_reduce_fusion.5, f32[16,8,3,128]{3,2,1,0:T(4,128)S(1)} %slice_add_fusion.50, ...), kind=kOutput, calls=%fused_computation.53.clone.1 | convolution fusion | flops 79937536 | bytes 9134084 | tf_op jit(solution)/shard_map/while/body/eval_jaxpr/gpij,gci->gpcj/dot_general | solution.py:56
  359.7 16.3 %scatter_fusion.1 = f32[256,3,128]{2,1,0:T(4,128)S(1)} fusion(f32[256,3,128]{2,1,0:T(4,128)S(1)} %broadcast.537, s32[256]{0:T(256)S(1)} %bitcast.218, f32[256,3,128]{2,1,0:T(4,128)} %bitcast.52), kind=kCustom, calls=%fused_computation.6 | custom fusion | bytes 1180672 | tf_op jit(solution)/shard_map/scatter | solution.py:189
  376.8 17.9 %all-to-all-start.4 = ((f32[32,8,3,128]{3,1,2,0:T(8,128)}), f32[32,8,3,128]{3,1,2,0:T(8,128)S(1)}, u32[]{:S(2)}, u32[]{:S(2)}) async-start(f32[32,8,3,128]{3,1,2,0:T(8,128)} %copy.88), calls=%async_computation.4 | async-start | bytes 786432 | tf_op jit(solution)/shard_map/all_to_all | solution.py:125
  396.1 11.9 %all-to-all-done.4 = f32[32,8,3,128]{3,1,2,0:T(8,128)S(1)} async-done(((f32[32,8,3,128]{3,1,2,0:T(8,128)}), f32[32,8,3,128]{3,1,2,0:T(8,128)S(1)}, u32[]{:S(2)}, u32[]{:S(2)}) %all-to-all-start.4) | async-done | bytes 393248 | tf_op jit(solution)/shard_map/all_to_all | solution.py:125
  (156 shorter events, 115.7 us)
Async XLA Ops:
  0.6 44.2 %copy-start.4 = (f32[3,32,5,128]{3,1,2,0:T(8,128)S(1)}, f32[3,32,5,128]{3,1,2,0:T(8,128)}, u32[]{:S(2)}) copy-start(f32[3,32,5,128]{3,1,2,0:T(8,128)} %param.13) | copy-start | bytes 737284
  4.0 14.4 %all-to-all-start = ((s32[32,1,8]{2,1,0:T(1,128)}), s32[32,1,8]{2,1,0:T(1,128)S(1)}, u32[]{:S(2)}, u32[]{:S(2)}) async-start(s32[32,1,8]{2,1,0:T(1,128)} %bitcast.28), calls=%async_computation | async-start | bytes 32768 | tf_op jit(solution)/shard_map/all_to_all | solution.py:155
  21.9 25.2 %all-to-all-start.1 = ((f32[32,8,6,128]{3,1,2,0:T(8,128)}), f32[32,8,6,128]{3,1,2,0:T(8,128)S(1)}, u32[]{:S(2)}, u32[]{:S(2)}) async-start(f32[32,8,6,128]{3,1,2,0:T(8,128)} %copy.73), calls=%async_computation.1 | async-start | bytes 1572864 | tf_op jit(solution)/shard_map/all_to_all | solution.py:119
  26.4 8.5 %collective-permute-start.1 = (f32[4,1,5,128]{3,1,2,0:T(1,128)S(1)}, f32[4,1,5,128]{3,1,2,0:T(1,128)S(1)}, u32[]{:S(2)}, u32[]{:S(2)}) collective-permute-start(f32[4,1,5,128]{3,1,2,0:T(1,128)S(1)} %get-tuple-element.231), channel_id=1, source_target_pairs={{8,0},{16,8},{24,16},{9,1},{17,9},{25,17},{10,2},{18,10},{26,18},{... | collective-permute-start | bytes 30728 | tf_op jit(solution)/shard_map/ppermute | solution.py:26
  27.7 10.3 %collective-permute-start = (f32[4,1,5,128]{3,1,2,0:T(1,128)S(1)}, f32[4,1,5,128]{3,1,2,0:T(1,128)S(1)}, u32[]{:S(2)}, u32[]{:S(2)}) collective-permute-start(f32[4,1,5,128]{3,1,2,0:T(1,128)S(1)} %get-tuple-element.230), channel_id=1, source_target_pairs={{0,8},{8,16},{16,24},{1,9},{9,17},{17,25},{2,10},{10,18},{18,26},{... | collective-permute-start | bytes 30728 | tf_op jit(solution)/shard_map/ppermute | solution.py:24
  39.1 4.5 %collective-permute-start.3 = (f32[4,34,5,1]{3,1,2,0:T(8,128)S(1)}, f32[4,34,5,1]{3,1,2,0:T(8,128)S(1)}, u32[]{:S(2)}, u32[]{:S(2)}) collective-permute-start(f32[4,34,5,1]{3,1,2,0:T(8,128)S(1)} %get-tuple-element.227), channel_id=1, source_target_pairs={{1,0},{2,1},{3,2},{4,3},{5,4},{6,5},{7,6},{9,8},{10,9},{11,10},{12... | collective-permute-start | bytes 8168 | tf_op jit(solution)/shard_map/ppermute | solution.py:26
  40.4 4.4 %collective-permute-start.2 = (f32[4,34,5,1]{3,1,2,0:T(8,128)S(1)}, f32[4,34,5,1]{3,1,2,0:T(8,128)S(1)}, u32[]{:S(2)}, u32[]{:S(2)}) collective-permute-start(f32[4,34,5,1]{3,1,2,0:T(8,128)S(1)} %get-tuple-element.226), channel_id=1, source_target_pairs={{0,1},{1,2},{2,3},{3,4},{4,5},{5,6},{6,7},{8,9},{9,10},{10,11},{11... | collective-permute-start | bytes 8168 | tf_op jit(solution)/shard_map/ppermute | solution.py:24
  45.3 1.0 copy-start.2
  165.7 37.9 %copy-start.3 = (f32[4,34,7,130]{3,1,2,0:T(8,128)S(1)}, f32[4,34,7,130]{3,1,2,0:T(8,128)}, u32[]{:S(2)}) copy-start(f32[4,34,7,130]{3,1,2,0:T(8,128)} %copy-done.2) | copy-start | bytes 1485124
  165.7 48.9 %copy-start.7 = (f32[32,5,128]{2,0,1:T(8,128)S(1)}, f32[32,5,128]{2,0,1:T(8,128)}, u32[]{:S(2)}) copy-start(f32[32,5,128]{2,0,1:T(8,128)} %broadcast_multiply_fusion) | copy-start | bytes 245764
  165.7 48.9 %copy-start.9 = (f32[3,32,5,128]{3,1,2,0:T(8,128)S(1)}, f32[3,32,5,128]{3,1,2,0:T(8,128)}, u32[]{:S(2)}) copy-start(f32[3,32,5,128]{3,1,2,0:T(8,128)} %param.14) | copy-start | bytes 737284
  182.9 31.2 %all-to-all-start.2 = ((f32[32,8,3,128]{3,1,2,0:T(8,128)}), f32[32,8,3,128]{3,1,2,0:T(8,128)S(1)}, u32[]{:S(2)}, u32[]{:S(2)}) async-start(f32[32,8,3,128]{3,1,2,0:T(8,128)} %copy.77), calls=%async_computation.2 | async-start | bytes 786432 | tf_op jit(solution)/shard_map/all_to_all | solution.py:125
  214.7 0.7 copy-start.5
  217.6 23.6 %all-to-all-start.3 = ((f32[32,8,6,128]{3,1,2,0:T(8,128)}), f32[32,8,6,128]{3,1,2,0:T(8,128)S(1)}, u32[]{:S(2)}, u32[]{:S(2)}) async-start(f32[32,8,6,128]{3,1,2,0:T(8,128)} %copy.83), calls=%async_computation.3 | async-start | bytes 1572864 | tf_op jit(solution)/shard_map/all_to_all | solution.py:119
  220.3 10.3 %collective-permute-start.5 = (f32[4,1,5,128]{3,1,0,2:T(1,128)S(1)}, f32[4,1,5,128]{3,1,0,2:T(1,128)S(1)}, u32[]{:S(2)}, u32[]{:S(2)}) collective-permute-start(f32[4,1,5,128]{3,1,0,2:T(1,128)S(1)} %get-tuple-element.229), channel_id=1, source_target_pairs={{8,0},{16,8},{24,16},{9,1},{17,9},{25,17},{10,2},{18,10},{26,18},{... | collective-permute-start | bytes 30728 | tf_op jit(solution)/shard_map/ppermute | solution.py:26
  221.6 12.2 %collective-permute-start.4 = (f32[4,1,5,128]{3,1,0,2:T(1,128)S(1)}, f32[4,1,5,128]{3,1,0,2:T(1,128)S(1)}, u32[]{:S(2)}, u32[]{:S(2)}) collective-permute-start(f32[4,1,5,128]{3,1,0,2:T(1,128)S(1)} %get-tuple-element.228), channel_id=1, source_target_pairs={{0,8},{8,16},{16,24},{1,9},{9,17},{17,25},{2,10},{10,18},{18,26},{... | collective-permute-start | bytes 30728 | tf_op jit(solution)/shard_map/ppermute | solution.py:24
  234.0 4.4 %collective-permute-start.7 = (f32[4,34,5,1]{3,1,0,2:T(8,128)S(1)}, f32[4,34,5,1]{3,1,0,2:T(8,128)S(1)}, u32[]{:S(2)}, u32[]{:S(2)}) collective-permute-start(f32[4,34,5,1]{3,1,0,2:T(8,128)S(1)} %get-tuple-element.225), channel_id=1, source_target_pairs={{1,0},{2,1},{3,2},{4,3},{5,4},{6,5},{7,6},{9,8},{10,9},{11,10},{12... | collective-permute-start | bytes 8168 | tf_op jit(solution)/shard_map/ppermute | solution.py:26
  235.3 4.4 %collective-permute-start.6 = (f32[4,34,5,1]{3,1,0,2:T(8,128)S(1)}, f32[4,34,5,1]{3,1,0,2:T(8,128)S(1)}, u32[]{:S(2)}, u32[]{:S(2)}) collective-permute-start(f32[4,34,5,1]{3,1,0,2:T(8,128)S(1)} %get-tuple-element.224), channel_id=1, source_target_pairs={{0,1},{1,2},{2,3},{3,4},{4,5},{5,6},{6,7},{8,9},{9,10},{10,11},{11... | collective-permute-start | bytes 8168 | tf_op jit(solution)/shard_map/ppermute | solution.py:24
  240.2 1.0 copy-start
  359.6 35.3 %copy-start.1 = (f32[4,34,7,130]{3,1,0,2:T(8,128)S(1)}, f32[4,34,7,130]{3,1,0,2:T(8,128)}, u32[]{:S(2)}) copy-start(f32[4,34,7,130]{3,1,0,2:T(8,128)} %copy-done) | copy-start | bytes 1485124
  359.6 48.8 %copy-start.6 = (f32[3,32,5,128]{3,1,0,2:T(8,128)S(1)}, f32[3,32,5,128]{3,1,0,2:T(8,128)}, u32[]{:S(2)}) copy-start(f32[3,32,5,128]{3,1,0,2:T(8,128)} %copy-done.5) | copy-start | bytes 737284
  359.6 48.8 %copy-start.8 = (f32[32,5,128]{2,0,1:T(8,128)S(1)}, f32[32,5,128]{2,0,1:T(8,128)}, u32[]{:S(2)}) copy-start(f32[32,5,128]{2,0,1:T(8,128)} %broadcast_multiply_fusion) | copy-start | bytes 245764
  376.8 31.1 %all-to-all-start.4 = ((f32[32,8,3,128]{3,1,2,0:T(8,128)}), f32[32,8,3,128]{3,1,2,0:T(8,128)S(1)}, u32[]{:S(2)}, u32[]{:S(2)}) async-start(f32[32,8,3,128]{3,1,2,0:T(8,128)} %copy.88), calls=%async_computation.4 | async-start | bytes 786432 | tf_op jit(solution)/shard_map/all_to_all | solution.py:125
where the time goes:
time: 417 us; the launch traced here: 410 us
  matrix products  147 us (35%)
  starting transfers between devices  68.8 us (16%)
  local copies, waits for them, and re-layouts  61.4 us (15%)
  loops' own time  54.1 us (13%)
  waiting for transfers between devices  40.8 us (10%)
  other arithmetic  36.7 us (9%)
    another operation x2, loops' own time, local(): lax.map(visit_group, (surface.reshape(group_count, group_size, 6, width_y...  54.1 us
    dot_general x4, matrix products, pair_forces(): jnp.einsum('gpij,gpcj->gpci', weights, far_vel, precision=highest)  52.6 us
    dot_general x4, matrix products, pair_forces(): jnp.einsum('gpij,gpcj->gpci', weights, far_disp, precision=highest)  52.4 us
    all_to_all x2, starting transfers between devices, deliver_reactions(): lax.all_to_all(shaped, ('gx', 'gy'), split_axis=0, concat_axis=0, tiled=T...  35.9 us
    scatter x2, local copies, waits for them, and re-layouts, local(): outgoing = jnp.zeros((requests, 3, width_y), jnp.float32).at[position].se...  32.6 us
    dot_general x4, matrix products, pair_forces(): jnp.einsum('gpij,gci->gpcj', weights, own_disp, precision=highest)  22.1 us
    all_to_all x2, waiting for transfers between devices, deliver_reactions(): lax.all_to_all(shaped, ('gx', 'gy'), split_axis=0, concat_axis=0, tiled=T...  21.2 us
    dot_general x4, matrix products, pair_forces(): jnp.einsum('gpij,gci->gpcj', weights, own_vel, precision=highest)  19.2 us
  transfers between devices with their start and end apart: 13, of which 9 were waited for; matrix products, arithmetic and copies ran while one was open for 3% of the time, Pallas kernels for 0%

commit v1 on v0

v1 whole, which is shorter than its diff:
```python
import math
import jax
import jax.numpy as jnp
from jax import lax
from jax.experimental import pallas as pl
from jax.experimental.pallas import tpu as pltpu
from jax.sharding import PartitionSpec as P

STEPS = 2

time_step = 0.2
penalty = 4.0
damping = 1.0
kernel_width = 4.0
frame_extent = 4.0

bf16 = jnp.bfloat16
f32 = jnp.float32


def with_halo(cells, sides, width):
    for axis, dim in sides:
        count = lax.axis_size(axis)
        ends = count - 1
        head = lax.slice_in_dim(cells, 0, width, axis=dim)
        tail = lax.slice_in_dim(cells, cells.shape[dim] - width, cells.shape[dim], axis=dim)
        cells = jnp.concatenate(
            [
                lax.ppermute(tail, axis, [(i, (i + 1) % count) for i in range(ends)]),
                cells,
                lax.ppermute(head, axis, [((i + 1) % count, i) for i in range(ends)]),
            ],
            axis=dim,
        )
    return cells


def internal_force(padded_disp, padded_stiff, displacement):
    size_x, size_z, size_y = displacement.shape[1:]
    s = padded_disp[:, 1:] + padded_disp[:, :-1]
    s = s[:, :, 1:] + s[:, :, :-1]
    s = s[:, :, :, 1:] + s[:, :, :, :-1]
    stiff = padded_stiff[: size_x + 1, : size_z + 1, : size_y + 1]
    w = jnp.concatenate([stiff[None] * (s * 0.125), stiff[None]], axis=0)
    w = w[:, 1:] + w[:, :-1]
    w = w[:, :, 1:] + w[:, :, :-1]
    w = w[:, :, :, 1:] + w[:, :, :, :-1]
    return w[:3] - displacement * w[3:]


def split3(x):
    a = x.astype(bf16).astype(f32)
    r = x - a
    b = r.astype(bf16).astype(f32)
    return a, b, r - b


def far_parts(x):
    a, b, c = split3(x)
    rhs = jnp.concatenate([a, b, a, b, c, a], axis=0).astype(bf16)
    lhs = jnp.concatenate([a, b, c, jnp.zeros_like(a)], axis=0).astype(bf16)
    return rhs, lhs


def contact_kernel(rev_row, rev_src, fwd, own_ref, all_ref, out_ref, own_t, acc):
    rows, width = own_ref.shape[0] // 8, own_ref.shape[1]
    row_id = lax.broadcasted_iota(jnp.int32, (8, width), 0)

    @pl.loop(0, rows)
    def _(r):
        x = own_ref[pl.ds(pl.multiple_of(r * 8, 8), 8), :]
        norm = jnp.broadcast_to(x[3:4], x.shape)
        y = jnp.where(row_id < 3, 2.0 * x, jnp.where(row_id == 3, 1.0, jnp.where(row_id == 4, norm, 0.0)))
        a, b, c = split3(y)
        pack = jnp.concatenate([a, a, b, b, a, c], axis=0)
        own_t[r] = pack.T.astype(bf16)

    def pairs(r, blocks):
        parts = [far_parts(all_ref[pl.ds(pl.multiple_of(b * 8, 8), 8), :]) for b in blocks]
        far = jnp.concatenate([p[0] for p in parts], axis=1)
        lhs = jnp.concatenate([p[1] for p in parts], axis=1)
        e = jnp.dot(own_t[r], far, preferred_element_type=f32)
        w = jnp.exp2(e)
        hi = w.astype(bf16)
        lo = (w - hi.astype(f32)).astype(bf16)
        dims = (((1,), (1,)), ((), ()))
        t = lax.dot_general(lhs, hi, dims, preferred_element_type=f32)
        t = t + lax.dot_general(lhs, lo, dims, preferred_element_type=f32)
        return t[0:8] + t[8:16] + t[16:24]

    per_row = fwd.shape[0] // rows

    @pl.loop(0, rows)
    def _(r):
        t = pairs(r, [fwd[r * per_row + k] for k in range(per_row)])
        acc[r] = t

    unroll = 8

    @pl.loop(0, rev_row.shape[0] // unroll)
    def _(g):
        got = []
        for k in range(unroll):
            r = rev_row[g * unroll + k]
            got.append((r, pairs(r, [rev_src[g * unroll + k]])))
        for r, t in got:
            acc[r] = acc[r] + t

    @pl.loop(0, rows)
    def _(r):
        x = own_ref[pl.ds(pl.multiple_of(r * 8, 8), 8), :]
        t = acc[r]
        out_ref[r] = x * t[4:5] - t


def contact_call(rev_row, rev_src, fwd, own, everyone):
    rows, width = own.shape[0] // 8, own.shape[1]
    smem = pl.BlockSpec(memory_space=pltpu.SMEM)
    vmem = pl.BlockSpec(memory_space=pltpu.VMEM)
    return pl.pallas_call(
        contact_kernel,
        out_shape=jax.ShapeDtypeStruct((rows, 8, width), f32),
        in_specs=[smem, smem, smem, vmem, vmem],
        out_specs=vmem,
        scratch_shapes=[
            pltpu.VMEM((rows, width, 48), bf16),
            pltpu.VMEM((rows, 8, width), f32),
        ],
        name="contact",
    )(rev_row, rev_src, fwd, own, everyone)


def local(displacement, velocity, stiffness, inverse_mass, facing):
    count_gx = lax.axis_size("gx")
    count_gy = lax.axis_size("gy")
    devices_all = count_gx * count_gy
    width_x, depth, width_y = stiffness.shape
    global_x = lax.axis_index("gx") * width_x + jnp.arange(width_x, dtype=jnp.int32)
    global_y = lax.axis_index("gy") * width_y + jnp.arange(width_y, dtype=jnp.int32)
    layer_index = jnp.arange(depth, dtype=jnp.int32)
    inside = (
        (global_x < width_x * count_gx - 1)[:, None, None]
        & (layer_index < depth - 1)[None, :, None]
        & (global_y < width_y * count_gy - 1)[None, None, :]
    )
    masked_stiff = jnp.where(inside, stiffness, 0.0)
    per_row = facing.shape[2]
    requests = per_row * width_x
    capacity = requests // devices_all
    me = lax.axis_index("gx") * count_gy + lax.axis_index("gy")
    wanted = facing.reshape(requests)
    wanted_x = wanted // count_gy
    fwd = (wanted_x // width_x * count_gy + wanted % count_gy) * width_x + wanted_x % width_x
    table = lax.all_gather(fwd, ("gx", "gy"))
    mine = table // width_x == me
    ordinal = jnp.arange(requests, dtype=jnp.int32)
    upto = (ordinal[:, None] <= ordinal[None, :]).astype(bf16)
    rank = jnp.dot(mine.astype(bf16), upto, preferred_element_type=f32)
    slot = (jnp.arange(capacity, dtype=jnp.int32) + 1).astype(f32)
    pick = mine[:, None, :] & (rank[:, None, :] == slot[None, :, None])
    rev_row = jnp.sum(jnp.where(pick, (table % width_x)[:, None, :], 0), axis=2).reshape(requests)
    source = jnp.arange(devices_all, dtype=jnp.int32)[:, None] * width_x + (ordinal // per_row)[None, :]
    rev_src = jnp.sum(jnp.where(pick, source[:, None, :], 0), axis=2).reshape(requests)

    place = (jnp.arange(width_y, dtype=f32) - (width_y - 1) / 2.0) * (frame_extent / width_y)
    frame = jnp.stack([jnp.zeros_like(place), place, jnp.zeros_like(place)], axis=0)[:, None, :]
    scale = math.sqrt(math.log2(math.e) / kernel_width)
    stiff_coef = penalty / (8.0 * width_y)
    damp_coef = damping / (8.0 * width_y)

    for repeat in range(STEPS):
        p = displacement[:, :, depth - 1, :] + frame
        q = stiff_coef * p - damp_coef * velocity[:, :, depth - 1, :]
        sp = scale * p
        norm = -jnp.sum(sp * sp, axis=0, keepdims=True)
        surface = jnp.concatenate([sp, norm, jnp.ones_like(norm), q], axis=0).transpose(1, 0, 2)
        surface = surface.reshape(width_x * 8, width_y)
        everyone = lax.all_gather(surface, ("gx", "gy"), tiled=True)
        stacked = jnp.concatenate([displacement, masked_stiff[None]], axis=0)
        padded = with_halo(stacked, (("gx", 1), ("gy", 3)), 1)
        padded = jnp.pad(padded, ((0, 0), (0, 0), (1, 1), (0, 0)))
        internal = internal_force(padded[:3], padded[3], displacement)
        contact = contact_call(rev_row, rev_src, fwd, surface, everyone)
        contact = contact[:, 5:8, :].transpose(1, 0, 2)
        total_force = internal.at[:, :, depth - 1, :].add(contact)
        velocity = velocity + time_step * inverse_mass[None] * total_force
        displacement = displacement + time_step * velocity
    return (displacement, velocity)


def solution(mesh):
    in_specs = (
        P(None, "gx", None, "gy"),
        P(None, "gx", None, "gy"),
        P("gx", None, "gy"),
        P("gx", None, "gy"),
        P("gx", "gy", None),
    )
    out_specs = (P(None, "gx", None, "gy"), P(None, "gx", None, "gy"))
    return jax.shard_map(local, mesh=mesh, in_specs=in_specs, out_specs=out_specs, check_vma=False)
```

time: 417 us -> 311 us (0.75)
  the two profiles are of different devices: /device:TPU:0 before, /device:TPU:9 now
where the time goes in v1:
time: 311 us; the launch traced here: 310 us
  Pallas kernels  139 us (45%)
  waiting for transfers between devices  82.2 us (26%)
  blocking collectives  32.4 us (10%)
  starting transfers between devices  24.2 us (8%)
  between operations  14.5 us (5%)
  other arithmetic  12.6 us (4%)
  local copies, waits for them, and re-layouts  4.36 us (1%)
    pallas_call x2, Pallas kernels, contact_call(): pl.pallas_call(contact_kernel, out_shape=jax.ShapeDtypeStruct((rows, 8, w...  139 us
    all_gather x2, waiting for transfers between devices, local(): everyone = lax.all_gather(surface, ('gx', 'gy'), tiled=True)  61.8 us
    all_gather x1, blocking collectives, local(): table = lax.all_gather(fwd, ('gx', 'gy'))  32.4 us
    ppermute x4, starting transfers between devices, with_halo(): lax.ppermute(tail, axis, [(i, (i + 1) % count) for i in range(ends)])  15.5 us
    ppermute x4, waiting for transfers between devices, with_halo(): lax.ppermute(head, axis, [((i + 1) % count, i) for i in range(ends)])  13.8 us
    ppermute x4, starting transfers between devices, with_halo(): lax.ppermute(head, axis, [((i + 1) % count, i) for i in range(ends)])  8.67 us
    ppermute x4, waiting for transfers between devices, with_halo(): lax.ppermute(tail, axis, [(i, (i + 1) % count) for i in range(ends)])  6.62 us
  transfers between devices with their start and end apart: 10, of which 8 were waited for; matrix products, arithmetic and copies ran while one was open for 2% of the time, Pallas kernels for 0%

profile of v1, /device:TPU:9, one launch (start us, length us, event | category | flops | bytes accessed | tf_op | source)
XLA Modules:
  0.0 309.5 jit_solution(10385395817948989200)
XLA Ops:
  7.3 1.0 select_bitcast_fusion
  9.2 1.9 collective-permute-start.1
  11.1 3.4 %collective-permute-start = (f32[4,1,5,128]{3,1,2,0:T(1,128)S(1)}, f32[4,1,5,128]{3,1,2,0:T(1,128)S(1)}, u32[]{:S(2)}, u32[]{:S(2)}) collective-permute-start(f32[4,1,5,128]{3,1,2,0:T(1,128)S(1)} %get-tuple-element.60), channel_id=1, source_target_pairs={{0,8},{8,16},{16,24},{1,9},{9,17},{17,25},{2,10},{10,18},{18,26},{... | collective-permute-start | bytes 30728 | tf_op jit(solution)/shard_map/ppermute | solution.py:29
  14.5 1.0 collective-permute-done
  15.5 1.0 fusion.17
  16.7 5.3 %collective-permute-start.2 = (f32[4,34,5,1]{3,1,2,0:T(8,128)S(1)}, f32[4,34,5,1]{3,1,2,0:T(8,128)S(1)}, u32[]{:S(2)}, u32[]{:S(2)}) collective-permute-start(f32[4,34,5,1]{3,1,2,0:T(8,128)S(1)} %get-tuple-element.48), channel_id=1, source_target_pairs={{0,1},{1,2},{2,3},{3,4},{4,5},{5,6},{6,7},{8,9},{9,10},{10,11},{11... | collective-permute-start | bytes 8168 | tf_op jit(solution)/shard_map/ppermute | solution.py:29
  22.0 1.9 collective-permute-start.3
  24.2 2.7 collective-permute-done.2
  26.9 6.0 %collective-permute-done.3 = f32[4,34,5,1]{3,1,2,0:T(8,128)S(1)} collective-permute-done((f32[4,34,5,1]{3,1,2,0:T(8,128)S(1)}, f32[4,34,5,1]{3,1,2,0:T(8,128)S(1)}, u32[]{:S(2)}, u32[]{:S(2)}) %collective-permute-start.3) | collective-permute-done | bytes 2752 | tf_op jit(solution)/shard_map/ppermute | solution.py:31
  36.9 32.4 %all-gather = s32[32,1,256]{2,1,0:T(1,128)S(1)} all-gather(s32[1,1,256]{2,1,0:T(1,128)S(1)} %fusion.45), channel_id=1, replica_groups=mesh['gx'=4,'gy'=8] {'gx','gy'}, dimensions={0}, use_global_device_ids=true | all-gather | bytes 33792 | tf_op jit(solution)/shard_map/all_gather | solution.py:154
  69.6 1.2 select_reduce_fusion
  72.7 25.5 %all-gather.4.cloned.1.call-done.all_ref = f32[8192,128]{1,0:T(8,128)} async-done(((f32[256,128]{1,0:T(8,128)}), f32[8192,128]{1,0:T(8,128)}) %all-gather.4.cloned.1.call-update) | async-done | bytes 4194320 | tf_op jit(solution)/shard_map/all_gather | solution.py:178
  98.3 69.5 %contact.2 = f32[32,8,128]{2,1,0:T(8,128)} custom-call(s32[256]{0:T(256)} %reshape.396.rev_row, s32[256]{0:T(256)} %reshape.397.rev_src, s32[256]{0:T(256)} %fusion.44.fwd, f32[256,128]{1,0:T(8,128)} %maximum_bitcast_fusion.own_ref, f32[8192,128]{1,0:T(8,128)} %all-gather.4.cloned.1.call-done.all_ref), custom_call_target="tpu_custom_call" | custom-call | tf_op jit(solution)/shard_map/contact/pallas_call | solution.py:120
  167.8 0.9 fusion.29
  170.1 2.4 collective-permute-start.4
  172.5 2.9 collective-permute-start.5
  175.4 1.5 collective-permute-done.5
  177.1 4.5 %collective-permute-start.6 = (f32[4,34,5,1]{3,1,2,0:T(8,128)S(1)}, f32[4,34,5,1]{3,1,2,0:T(8,128)S(1)}, u32[]{:S(2)}, u32[]{:S(2)}) collective-permute-start(f32[4,34,5,1]{3,1,2,0:T(8,128)S(1)} %get-tuple-element.46), channel_id=1, source_target_pairs={{0,1},{1,2},{2,3},{3,4},{4,5},{5,6},{6,7},{8,9},{9,10},{10,11},{11... | collective-permute-start | bytes 8168 | tf_op jit(solution)/shard_map/ppermute | solution.py:29
  181.6 1.9 collective-permute-start.7
  183.5 2.9 collective-permute-done.6
  186.5 6.2 %collective-permute-done.7 = f32[4,34,5,1]{3,1,2,0:T(8,128)S(1)} collective-permute-done((f32[4,34,5,1]{3,1,2,0:T(8,128)S(1)}, f32[4,34,5,1]{3,1,2,0:T(8,128)S(1)}, u32[]{:S(2)}, u32[]{:S(2)}) %collective-permute-start.7) | collective-permute-done | bytes 2752 | tf_op jit(solution)/shard_map/ppermute | solution.py:31
  194.3 36.3 %all-gather.6.cloned.1.call-done.all_ref = f32[8192,128]{1,0:T(8,128)} async-done(((f32[256,128]{1,0:T(8,128)}), f32[8192,128]{1,0:T(8,128)}) %all-gather.6.cloned.1.call-update) | async-done | bytes 4194320 | tf_op jit(solution)/shard_map/all_gather | solution.py:178
  230.6 69.5 %contact.3 = f32[32,8,128]{2,1,0:T(8,128)} custom-call(s32[256]{0:T(256)} %reshape.396.rev_row, s32[256]{0:T(256)} %reshape.397.rev_src, s32[256]{0:T(256)} %fusion.44.fwd, f32[256,128]{1,0:T(8,128)} %maximum_bitcast_fusion.1.own_ref, f32[8192,128]{1,0:T(8,128)} %all-gather.6.cloned.1.call-done.all_ref), custom_call_target="tpu_custom_call" | custom-call | tf_op jit(solution)/shard_map/contact/pallas_call | solution.py:120
  300.1 0.9 fusion.24
  (79 shorter events, 12.2 us)
Async XLA Ops:
  7.2 91.1 %all-gather.4.cloned.1.call-start = ((), (), s32[]{:S(2)}) async-start(), calls=%async_computation | async-start | bytes 4325376 | tf_op jit(solution)/shard_map/all_gather | solution.py:178
  9.2 5.3 %collective-permute-start.1 = (f32[4,1,5,128]{3,1,2,0:T(1,128)S(1)}, f32[4,1,5,128]{3,1,2,0:T(1,128)S(1)}, u32[]{:S(2)}, u32[]{:S(2)}) collective-permute-start(f32[4,1,5,128]{3,1,2,0:T(1,128)S(1)} %get-tuple-element.44), channel_id=1, source_target_pairs={{8,0},{16,8},{24,16},{9,1},{17,9},{25,17},{10,2},{18,10},{26,18},{... | collective-permute-start | bytes 30728 | tf_op jit(solution)/shard_map/ppermute | solution.py:31
  11.1 4.4 %collective-permute-start = (f32[4,1,5,128]{3,1,2,0:T(1,128)S(1)}, f32[4,1,5,128]{3,1,2,0:T(1,128)S(1)}, u32[]{:S(2)}, u32[]{:S(2)}) collective-permute-start(f32[4,1,5,128]{3,1,2,0:T(1,128)S(1)} %get-tuple-element.60), channel_id=1, source_target_pairs={{0,8},{8,16},{16,24},{1,9},{9,17},{17,25},{2,10},{10,18},{18,26},{... | collective-permute-start | bytes 30728 | tf_op jit(solution)/shard_map/ppermute | solution.py:29
  14.5 9.5 %copy-start.1 = (f32[3,32,5,128]{3,1,2,0:T(8,128)S(1)}, f32[3,32,5,128]{3,1,2,0:T(8,128)}, u32[]{:S(2)}) copy-start(f32[3,32,5,128]{3,1,2,0:T(8,128)} %param.10) | copy-start | bytes 737284
  16.5 16.4 %copy-start = (f32[3,32,5,128]{3,1,2,0:T(8,128)S(1)}, f32[3,32,5,128]{3,1,2,0:T(8,128)}, u32[]{:S(2)}) copy-start(f32[3,32,5,128]{3,1,2,0:T(8,128)} %param.9) | copy-start | bytes 737284
  16.7 10.1 %collective-permute-start.2 = (f32[4,34,5,1]{3,1,2,0:T(8,128)S(1)}, f32[4,34,5,1]{3,1,2,0:T(8,128)S(1)}, u32[]{:S(2)}, u32[]{:S(2)}) collective-permute-start(f32[4,34,5,1]{3,1,2,0:T(8,128)S(1)} %get-tuple-element.48), channel_id=1, source_target_pairs={{0,1},{1,2},{2,3},{3,4},{4,5},{5,6},{6,7},{8,9},{9,10},{10,11},{11... | collective-permute-start | bytes 8168 | tf_op jit(solution)/shard_map/ppermute | solution.py:29
  22.0 10.9 %collective-permute-start.3 = (f32[4,34,5,1]{3,1,2,0:T(8,128)S(1)}, f32[4,34,5,1]{3,1,2,0:T(8,128)S(1)}, u32[]{:S(2)}, u32[]{:S(2)}) collective-permute-start(f32[4,34,5,1]{3,1,2,0:T(8,128)S(1)} %get-tuple-element.49), channel_id=1, source_target_pairs={{1,0},{2,1},{3,2},{4,3},{5,4},{6,5},{7,6},{9,8},{10,9},{11,10},{12... | collective-permute-start | bytes 8168 | tf_op jit(solution)/shard_map/ppermute | solution.py:31
  35.3 1.3 copy-start.3
  35.4 37.3 %copy-start.2 = (f32[32,5,128]{2,0,1:T(8,128)S(1)}, f32[32,5,128]{2,0,1:T(8,128)}, u32[]{:S(2)}) copy-start(f32[32,5,128]{2,0,1:T(8,128)} %param.12) | copy-start | bytes 245764
  36.5 194.1 %all-gather.6.cloned.1.call-start = ((), (), s32[]{:S(2)}) async-start(), calls=%async_computation.1 | async-start | bytes 4325376 | tf_op jit(solution)/shard_map/all_gather | solution.py:178
  170.1 5.3 %collective-permute-start.4 = (f32[4,1,5,128]{3,1,2,0:T(1,128)S(1)}, f32[4,1,5,128]{3,1,2,0:T(1,128)S(1)}, u32[]{:S(2)}, u32[]{:S(2)}) collective-permute-start(f32[4,1,5,128]{3,1,2,0:T(1,128)S(1)} %get-tuple-element.56), channel_id=1, source_target_pairs={{0,8},{8,16},{16,24},{1,9},{9,17},{17,25},{2,10},{10,18},{18,26},{... | collective-permute-start | bytes 30728 | tf_op jit(solution)/shard_map/ppermute | solution.py:29
  172.5 4.4 %collective-permute-start.5 = (f32[4,1,5,128]{3,1,2,0:T(1,128)S(1)}, f32[4,1,5,128]{3,1,2,0:T(1,128)S(1)}, u32[]{:S(2)}, u32[]{:S(2)}) collective-permute-start(f32[4,1,5,128]{3,1,2,0:T(1,128)S(1)} %get-tuple-element.57), channel_id=1, source_target_pairs={{8,0},{16,8},{24,16},{9,1},{17,9},{25,17},{10,2},{18,10},{26,18},{... | collective-permute-start | bytes 30728 | tf_op jit(solution)/shard_map/ppermute | solution.py:31
  177.1 9.3 %collective-permute-start.6 = (f32[4,34,5,1]{3,1,2,0:T(8,128)S(1)}, f32[4,34,5,1]{3,1,2,0:T(8,128)S(1)}, u32[]{:S(2)}, u32[]{:S(2)}) collective-permute-start(f32[4,34,5,1]{3,1,2,0:T(8,128)S(1)} %get-tuple-element.46), channel_id=1, source_target_pairs={{0,1},{1,2},{2,3},{3,4},{4,5},{5,6},{6,7},{8,9},{9,10},{10,11},{11... | collective-permute-start | bytes 8168 | tf_op jit(solution)/shard_map/ppermute | solution.py:29
  181.6 11.1 %collective-permute-start.7 = (f32[4,34,5,1]{3,1,2,0:T(8,128)S(1)}, f32[4,34,5,1]{3,1,2,0:T(8,128)S(1)}, u32[]{:S(2)}, u32[]{:S(2)}) collective-permute-start(f32[4,34,5,1]{3,1,2,0:T(8,128)S(1)} %get-tuple-element.47), channel_id=1, source_target_pairs={{1,0},{2,1},{3,2},{4,3},{5,4},{6,5},{7,6},{9,8},{10,9},{11,10},{12... | collective-permute-start | bytes 8168 | tf_op jit(solution)/shard_map/ppermute | solution.py:31
Sparse Core Ops, SparseCore 0:
  36.7 61.5 all-gather.3
  170.2 60.3 all-gather.5

commit v2 on v1

--- a/solution.py
+++ b/solution.py
@@ -1,3 +1,4 @@
+import functools
 import math
 import jax
 import jax.numpy as jnp
@@ -128,6 +129,97 @@
         ],
         name="contact",
     )(rev_row, rev_src, fwd, own, everyone)
+
+
+def gather_kernel(count_gx, count_gy, own, out, local_sem, send_sems, recv_sems):
+    gx = lax.axis_index("gx")
+    gy = lax.axis_index("gy")
+    bits = count_gy.bit_length() - 1
+    flips = [(1 - 2 * ((gy // (1 << k)) % 2)) * (1 << k) for k in range(bits)]
+    side = gy % 2
+    middle = list(range(1, bits))
+    steps = [side * flips[b] + (1 - side) * flips[a] for a, b in zip(middle, middle[::-1])]
+    steps.append(flips[0])
+
+    peers = [(lax.rem(gx + k, count_gx), gy) for k in range(1, count_gx)]
+    peers += [(gx, gy + step) for step in steps]
+    barrier = pltpu.get_barrier_semaphore()
+    for peer in peers:
+        pl.semaphore_signal(barrier, inc=1, device_id=peer, device_id_type=pl.DeviceIdType.MESH)
+    pl.semaphore_wait(barrier, len(peers))
+
+    here = gx * count_gy + gy
+    keep = pltpu.make_async_copy(own, out.at[here], local_sem)
+    keep.start()
+    started = []
+
+    def send(slot, peer):
+        copy = pltpu.make_async_remote_copy(
+            src_ref=own if slot is None else out.at[slot],
+            dst_ref=out.at[here if slot is None else slot],
+            send_sem=send_sems.at[len(started)],
+            recv_sem=recv_sems.at[here if slot is None else slot],
+            device_id=peer,
+            device_id_type=pl.DeviceIdType.MESH,
+        )
+        copy.start()
+        started.append(copy)
+
+    def arrived(slot):
+        pltpu.make_async_remote_copy(
+            src_ref=own,
+            dst_ref=out.at[slot],
+            send_sem=send_sems.at[0],
+            recv_sem=recv_sems.at[slot],
+            device_id=peers[0],
+            device_id_type=pl.DeviceIdType.MESH,
+        ).wait_recv()
+
+    for peer in peers:
+        send(None, peer)
+    half = 1 << (bits - 1)
+    waves = [(k, m) for total in range(count_gx + half - 1) for m in range(half)
+             for k in [total - m] if 0 <= k < count_gx and (k, m) != (0, 0)]
+    for k, m in waves:
+        column = gy
+        for b in range(bits - 1):
+            if m >> b & 1:
+                column = column + steps[b]
+        slot = lax.rem(gx + k, count_gx) * count_gy + column
+        arrived(slot)
+        for b in range(m.bit_length(), bits):
+            send(slot, (gx, gy + steps[b]))
+    for k, m in [(0, 0)] + waves:
+        column = gy + flips[0]
+        for b in range(bits - 1):
+            if m >> b & 1:
+                column = column + steps[bits - 2 - b]
+        arrived(lax.rem(gx + k, count_gx) * count_gy + column)
+    keep.wait()
+    for copy in started:
+        copy.wait_send()
+
+
+def gather_call(own, count_gx, count_gy):
+    devices_all = count_gx * count_gy
+    bits = count_gy.bit_length() - 1
+    half = count_gy // 2
+    sends = count_gx - 1 + bits
+    for m in range(half):
+        sends += (count_gx - (m == 0)) * (bits - m.bit_length())
+    return pl.pallas_call(
+        functools.partial(gather_kernel, count_gx, count_gy),
+        out_shape=jax.ShapeDtypeStruct((devices_all,) + own.shape, f32),
+        in_specs=[pl.BlockSpec(memory_space=pltpu.VMEM)],
+        out_specs=pl.BlockSpec(memory_space=pl.ANY),
+        scratch_shapes=[
+            pltpu.SemaphoreType.DMA,
+            pltpu.SemaphoreType.DMA((sends,)),
+            pltpu.SemaphoreType.DMA((devices_all,)),
+        ],
+        compiler_params=pltpu.CompilerParams(collective_id=0, has_side_effects=True),
+        name="gather",
+    )(own)
 
 
 def local(displacement, velocity, stiffness, inverse_mass, facing):
@@ -149,19 +241,10 @@
     capacity = requests // devices_all
     me = lax.axis_index("gx") * count_gy + lax.axis_index("gy")
     wanted = facing.reshape(requests)
+    extra = -(-requests // (8 * width_y))
+    unit = width_x + extra
     wanted_x = wanted // count_gy
-    fwd = (wanted_x // width_x * count_gy + wanted % count_gy) * width_x + wanted_x % width_x
-    table = lax.all_gather(fwd, ("gx", "gy"))
-    mine = table // width_x == me
-    ordinal = jnp.arange(requests, dtype=jnp.int32)
-    upto = (ordinal[:, None] <= ordinal[None, :]).astype(bf16)
-    rank = jnp.dot(mine.astype(bf16), upto, preferred_element_type=f32)
-    slot = (jnp.arange(capacity, dtype=jnp.int32) + 1).astype(f32)
-    pick = mine[:, None, :] & (rank[:, None, :] == slot[None, :, None])
-    rev_row = jnp.sum(jnp.where(pick, (table % width_x)[:, None, :], 0), axis=2).reshape(requests)
-    source = jnp.arange(devices_all, dtype=jnp.int32)[:, None] * width_x + (ordinal // per_row)[None, :]
-    rev_src = jnp.sum(jnp.where(pick, source[:, None, :], 0), axis=2).reshape(requests)
-
+    fwd = (wanted_x // width_x * count_gy + wanted % count_gy) * unit + wanted_x % width_x
     place = (jnp.arange(width_y, dtype=f32) - (width_y - 1) / 2.0) * (frame_extent / width_y)
     frame = jnp.stack([jnp.zeros_like(place), place, jnp.zeros_like(place)], axis=0)[:, None, :]
     scale = math.sqrt(math.log2(math.e) / kernel_width)
@@ -175,7 +258,20 @@
         norm = -jnp.sum(sp * sp, axis=0, keepdims=True)
         surface = jnp.concatenate([sp, norm, jnp.ones_like(norm), q], axis=0).transpose(1, 0, 2)
         surface = surface.reshape(width_x * 8, width_y)
-        everyone = lax.all_gather(surface, ("gx", "gy"), tiled=True)
+        tail = jnp.pad(fwd.astype(f32), (0, extra * 8 * width_y - requests)).reshape(extra * 8, width_y)
+        everyone = gather_call(jnp.concatenate([surface, tail], axis=0), count_gx, count_gy)
+        if repeat == 0:
+            table = everyone[:, width_x * 8 :].reshape(devices_all, -1)[:, :requests].astype(jnp.int32)
+            mine = table // unit == me
+            ordinal = jnp.arange(requests, dtype=jnp.int32)
+            upto = (ordinal[:, None] <= ordinal[None, :]).astype(bf16)
+            rank = jnp.dot(mine.astype(bf16), upto, preferred_element_type=f32)
+            slot = (jnp.arange(capacity, dtype=jnp.int32) + 1).astype(f32)
+            pick = mine[:, None, :] & (rank[:, None, :] == slot[None, :, None])
+            rev_row = jnp.sum(jnp.where(pick, (table % unit)[:, None, :], 0), axis=2).reshape(requests)
+            source = jnp.arange(devices_all, dtype=jnp.int32)[:, None] * unit + (ordinal // per_row)[None, :]
+            rev_src = jnp.sum(jnp.where(pick, source[:, None, :], 0), axis=2).reshape(requests)
+        everyone = everyone.reshape(-1, width_y)
         stacked = jnp.concatenate([displacement, masked_stiff[None]], axis=0)
         padded = with_halo(stacked, (("gx", 1), ("gy", 3)), 1)
         padded = jnp.pad(padded, ((0, 0), (0, 0), (1, 1), (0, 0)))

time: 311 us -> 263 us (0.85)
  waiting for transfers between devices: 82.2 us -> 9.66 us
  Pallas kernels: 139 us -> 209 us
  blocking collectives: 32.4 us -> 0 us
  between operations: 14.5 us -> 1.18 us
    pallas_call x0 -> x2, Pallas kernels: none -> 70.3 us  [gather_call(): pl.pallas_call(functools.partial(gather_kernel, count_gx, count_gy), out_...]
    all_gather x2 -> x0, waiting for transfers between devices: 61.8 us -> none  [local(): everyone = lax.all_gather(surface, ('gx', 'gy'), tiled=True)]
    all_gather x1 -> x0, blocking collectives: 32.4 us -> none  [local(): table = lax.all_gather(fwd, ('gx', 'gy'))]
    ppermute x4, waiting for transfers between devices: 13.8 us -> 6.99 us  [with_halo(): lax.ppermute(head, axis, [((i + 1) % count, i) for i in range(ends)])]
    ppermute x4, waiting for transfers between devices: 6.62 us -> 2.67 us  [with_halo(): lax.ppermute(tail, axis, [(i, (i + 1) % count) for i in range(ends)])]
  transfers between devices with their start and end apart: 10 -> 8, of which waited for: 8 -> 3; matrix products, arithmetic and copies ran while one was open for 2% -> 1% of each run, Pallas kernels for 0% -> 40%
where the time goes in v2:
time: 263 us; the launch traced here: 262 us
  Pallas kernels  209 us (79%)
  starting transfers between devices  22.8 us (9%)
  other arithmetic  12.7 us (5%)
  waiting for transfers between devices  9.66 us (4%)
  local copies, waits for them, and re-layouts  6.4 us (2%)
    pallas_call x2, Pallas kernels, contact_call(): pl.pallas_call(contact_kernel, out_shape=jax.ShapeDtypeStruct((rows, 8, w...  139 us
    pallas_call x2, Pallas kernels, gather_call(): pl.pallas_call(functools.partial(gather_kernel, count_gx, count_gy), out_...  70.3 us
    ppermute x4, starting transfers between devices, with_halo(): lax.ppermute(tail, axis, [(i, (i + 1) % count) for i in range(ends)])  13.5 us
    ppermute x4, starting transfers between devices, with_halo(): lax.ppermute(head, axis, [((i + 1) % count, i) for i in range(ends)])  9.27 us
    ppermute x4, waiting for transfers between devices, with_halo(): lax.ppermute(head, axis, [((i + 1) % count, i) for i in range(ends)])  6.99 us
  transfers between devices with their start and end apart: 8, of which 3 were waited for; matrix products, arithmetic and copies ran while one was open for 1% of the time, Pallas kernels for 40%

profile of v2, /device:TPU:9, one launch (start us, length us, event | category | flops | bytes accessed | tf_op | source)
XLA Modules:
  0.0 262.3 jit_solution(2434056240329987039)
XLA Ops:
  0.8 1.0 select_bitcast_fusion
  1.7 0.9 pad_maximum_fusion.9
  2.6 3.2 %collective-permute-start = (f32[4,1,5,128]{3,1,2,0:T(1,128)S(1)}, f32[4,1,5,128]{3,1,2,0:T(1,128)S(1)}, u32[]{:S(2)}, u32[]{:S(2)}) collective-permute-start(f32[4,1,5,128]{3,1,2,0:T(1,128)S(1)} %get-tuple-element.62), channel_id=1, source_target_pairs={{0,8},{8,16},{16,24},{1,9},{9,17},{17,25},{2,10},{10,18},{18,26},{... | collective-permute-start | bytes 30728 | tf_op jit(solution)/shard_map/ppermute | solution.py:30
  5.8 2.1 collective-permute-start.1
  7.9 0.8 copy.32
  9.4 0.9 broadcast_multiply_fusion.1
  10.4 1.1 fusion.17
  11.6 4.9 %collective-permute-start.2 = (f32[4,34,5,1]{3,1,2,0:T(8,128)S(1)}, f32[4,34,5,1]{3,1,2,0:T(8,128)S(1)}, u32[]{:S(2)}, u32[]{:S(2)}) collective-permute-start(f32[4,34,5,1]{3,1,2,0:T(8,128)S(1)} %get-tuple-element.50), channel_id=1, source_target_pairs={{0,1},{1,2},{2,3},{3,4},{4,5},{5,6},{6,7},{8,9},{9,10},{10,11},{11... | collective-permute-start | bytes 8168 | tf_op jit(solution)/shard_map/ppermute | solution.py:30
  16.6 1.9 collective-permute-start.3
  18.8 2.7 %collective-permute-done.2 = f32[4,34,5,1]{3,1,2,0:T(8,128)S(1)} collective-permute-done((f32[4,34,5,1]{3,1,2,0:T(8,128)S(1)}, f32[4,34,5,1]{3,1,2,0:T(8,128)S(1)}, u32[]{:S(2)}, u32[]{:S(2)}) %collective-permute-start.2) | collective-permute-done | bytes 2752 | tf_op jit(solution)/shard_map/ppermute | solution.py:30
  21.4 6.0 %collective-permute-done.3 = f32[4,34,5,1]{3,1,2,0:T(8,128)S(1)} collective-permute-done((f32[4,34,5,1]{3,1,2,0:T(8,128)S(1)}, f32[4,34,5,1]{3,1,2,0:T(8,128)S(1)}, u32[]{:S(2)}, u32[]{:S(2)}) %collective-permute-start.3) | collective-permute-done | bytes 2752 | tf_op jit(solution)/shard_map/ppermute | solution.py:32
  31.1 34.6 %gather.2 = f32[32,264,128]{2,1,0:T(8,128)} custom-call(f32[264,128]{1,0:T(8,128)} %pad_maximum_fusion.7.own), custom_call_target="tpu_custom_call" | custom-call | tf_op jit(solution)/shard_map/gather/pallas_call | solution.py:210
  65.7 0.9 slice.227
  66.9 1.2 select_reduce_fusion
  69.5 69.6 %contact.2 = f32[32,8,128]{2,1,0:T(8,128)} custom-call(s32[256]{0:T(256)} %reshape.239.rev_row, s32[256]{0:T(256)} %reshape.240.rev_src, s32[256]{0:T(256)} %get-tuple-element.45.fwd, f32[256,128]{1,0:T(8,128)} %copy-done.1, f32[8448,128]{1,0:T(8,128)} %bitcast.77), custom_call_target="tpu_custom_call" | custom-call | tf_op jit(solution)/shard_map/contact/pallas_call | solution.py:121
  139.1 0.9 fusion.29
  140.6 1.9 collective-permute-start.4
  142.5 3.4 %collective-permute-start.5 = (f32[4,1,5,128]{3,1,2,0:T(1,128)S(1)}, f32[4,1,5,128]{3,1,2,0:T(1,128)S(1)}, u32[]{:S(2)}, u32[]{:S(2)}) collective-permute-start(f32[4,1,5,128]{3,1,2,0:T(1,128)S(1)} %get-tuple-element.59), channel_id=1, source_target_pairs={{8,0},{16,8},{24,16},{9,1},{17,9},{25,17},{10,2},{18,10},{26,18},{... | collective-permute-start | bytes 30728 | tf_op jit(solution)/shard_map/ppermute | solution.py:32
  146.0 0.9 collective-permute-done.5
  147.2 3.5 %collective-permute-start.6 = (f32[4,34,5,1]{3,1,2,0:T(8,128)S(1)}, f32[4,34,5,1]{3,1,2,0:T(8,128)S(1)}, u32[]{:S(2)}, u32[]{:S(2)}) collective-permute-start(f32[4,34,5,1]{3,1,2,0:T(8,128)S(1)} %get-tuple-element.48), channel_id=1, source_target_pairs={{0,1},{1,2},{2,3},{3,4},{4,5},{5,6},{6,7},{8,9},{9,10},{10,11},{11... | collective-permute-start | bytes 8168 | tf_op jit(solution)/shard_map/ppermute | solution.py:30
  150.7 1.9 collective-permute-start.7
  153.3 35.7 %gather.3 = f32[32,264,128]{2,1,0:T(8,128)} custom-call(f32[264,128]{1,0:T(8,128)} %pad_maximum_fusion.6.own), custom_call_target="tpu_custom_call" | custom-call | tf_op jit(solution)/shard_map/gather/pallas_call | solution.py:210
  189.0 69.6 %contact.3 = f32[32,8,128]{2,1,0:T(8,128)} custom-call(s32[256]{0:T(256)} %reshape.239.rev_row, s32[256]{0:T(256)} %reshape.240.rev_src, s32[256]{0:T(256)} %get-tuple-element.45.fwd, f32[256,128]{1,0:T(8,128)} %copy-done.2, f32[8448,128]{1,0:T(8,128)} %bitcast.78), custom_call_target="tpu_custom_call" | custom-call | tf_op jit(solution)/shard_map/contact/pallas_call | solution.py:121
  260.8 0.7 copy.37
  (78 shorter events, 10.9 us)
Async XLA Ops:
  2.6 7.7 %collective-permute-start = (f32[4,1,5,128]{3,1,2,0:T(1,128)S(1)}, f32[4,1,5,128]{3,1,2,0:T(1,128)S(1)}, u32[]{:S(2)}, u32[]{:S(2)}) collective-permute-start(f32[4,1,5,128]{3,1,2,0:T(1,128)S(1)} %get-tuple-element.62), channel_id=1, source_target_pairs={{0,8},{8,16},{16,24},{1,9},{9,17},{17,25},{2,10},{10,18},{18,26},{... | collective-permute-start | bytes 30728 | tf_op jit(solution)/shard_map/ppermute | solution.py:30
  5.8 4.5 %collective-permute-start.1 = (f32[4,1,5,128]{3,1,2,0:T(1,128)S(1)}, f32[4,1,5,128]{3,1,2,0:T(1,128)S(1)}, u32[]{:S(2)}, u32[]{:S(2)}) collective-permute-start(f32[4,1,5,128]{3,1,2,0:T(1,128)S(1)} %get-tuple-element.46), channel_id=1, source_target_pairs={{8,0},{16,8},{24,16},{9,1},{17,9},{25,17},{10,2},{18,10},{26,18},{... | collective-permute-start | bytes 30728 | tf_op jit(solution)/shard_map/ppermute | solution.py:32
  10.3 8.2 %copy-start.3 = (f32[3,32,5,128]{3,1,2,0:T(8,128)S(1)}, f32[3,32,5,128]{3,1,2,0:T(8,128)}, u32[]{:S(2)}) copy-start(f32[3,32,5,128]{3,1,2,0:T(8,128)} %param.10) | copy-start | bytes 737284
  11.4 16.0 %copy-start = (f32[3,32,5,128]{3,1,2,0:T(8,128)S(1)}, f32[3,32,5,128]{3,1,2,0:T(8,128)}, u32[]{:S(2)}) copy-start(f32[3,32,5,128]{3,1,2,0:T(8,128)} %param.9) | copy-start | bytes 737284
  11.6 9.8 %collective-permute-start.2 = (f32[4,34,5,1]{3,1,2,0:T(8,128)S(1)}, f32[4,34,5,1]{3,1,2,0:T(8,128)S(1)}, u32[]{:S(2)}, u32[]{:S(2)}) collective-permute-start(f32[4,34,5,1]{3,1,2,0:T(8,128)S(1)} %get-tuple-element.50), channel_id=1, source_target_pairs={{0,1},{1,2},{2,3},{3,4},{4,5},{5,6},{6,7},{8,9},{9,10},{10,11},{11... | collective-permute-start | bytes 8168 | tf_op jit(solution)/shard_map/ppermute | solution.py:30
  16.6 10.9 %collective-permute-start.3 = (f32[4,34,5,1]{3,1,2,0:T(8,128)S(1)}, f32[4,34,5,1]{3,1,2,0:T(8,128)S(1)}, u32[]{:S(2)}, u32[]{:S(2)}) collective-permute-start(f32[4,34,5,1]{3,1,2,0:T(8,128)S(1)} %get-tuple-element.51), channel_id=1, source_target_pairs={{1,0},{2,1},{3,2},{4,3},{5,4},{6,5},{7,6},{9,8},{10,9},{11,10},{12... | collective-permute-start | bytes 8168 | tf_op jit(solution)/shard_map/ppermute | solution.py:32
  30.4 35.3 %copy-start.1 = (f32[256,128]{1,0:T(8,128)}, f32[256,128]{1,0:T(8,128)S(1)}, u32[]{:S(2)}) copy-start(f32[256,128]{1,0:T(8,128)S(1)} %maximum_bitcast_fusion.own_ref) | copy-start | bytes 393220
  140.6 5.4 %collective-permute-start.4 = (f32[4,1,5,128]{3,1,2,0:T(1,128)S(1)}, f32[4,1,5,128]{3,1,2,0:T(1,128)S(1)}, u32[]{:S(2)}, u32[]{:S(2)}) collective-permute-start(f32[4,1,5,128]{3,1,2,0:T(1,128)S(1)} %get-tuple-element.58), channel_id=1, source_target_pairs={{0,8},{8,16},{16,24},{1,9},{9,17},{17,25},{2,10},{10,18},{18,26},{... | collective-permute-start | bytes 30728 | tf_op jit(solution)/shard_map/ppermute | solution.py:30
  142.5 4.4 %collective-permute-start.5 = (f32[4,1,5,128]{3,1,2,0:T(1,128)S(1)}, f32[4,1,5,128]{3,1,2,0:T(1,128)S(1)}, u32[]{:S(2)}, u32[]{:S(2)}) collective-permute-start(f32[4,1,5,128]{3,1,2,0:T(1,128)S(1)} %get-tuple-element.59), channel_id=1, source_target_pairs={{8,0},{16,8},{24,16},{9,1},{17,9},{25,17},{10,2},{18,10},{26,18},{... | collective-permute-start | bytes 30728 | tf_op jit(solution)/shard_map/ppermute | solution.py:32
  146.0 6.6 %copy-start.2 = (f32[256,128]{1,0:T(8,128)}, f32[256,128]{1,0:T(8,128)S(1)}, u32[]{:S(2)}) copy-start(f32[256,128]{1,0:T(8,128)S(1)} %maximum_bitcast_fusion.1.own_ref) | copy-start | bytes 393220
  147.2 111.3 %collective-permute-start.6 = (f32[4,34,5,1]{3,1,2,0:T(8,128)S(1)}, f32[4,34,5,1]{3,1,2,0:T(8,128)S(1)}, u32[]{:S(2)}, u32[]{:S(2)}) collective-permute-start(f32[4,34,5,1]{3,1,2,0:T(8,128)S(1)} %get-tuple-element.48), channel_id=1, source_target_pairs={{0,1},{1,2},{2,3},{3,4},{4,5},{5,6},{6,7},{8,9},{9,10},{10,11},{11... | collective-permute-start | bytes 8168 | tf_op jit(solution)/shard_map/ppermute | solution.py:30
  150.7 107.9 %collective-permute-start.7 = (f32[4,34,5,1]{3,1,2,0:T(8,128)S(1)}, f32[4,34,5,1]{3,1,2,0:T(8,128)S(1)}, u32[]{:S(2)}, u32[]{:S(2)}) collective-permute-start(f32[4,34,5,1]{3,1,2,0:T(8,128)S(1)} %get-tuple-element.49), channel_id=1, source_target_pairs={{1,0},{2,1},{3,2},{4,3},{5,4},{6,5},{7,6},{9,8},{10,9},{11,10},{12... | collective-permute-start | bytes 8168 | tf_op jit(solution)/shard_map/ppermute | solution.py:32
  259.7 0.9 copy-start.4

commit v3 on v2

--- a/solution.py
+++ b/solution.py
@@ -83,20 +83,18 @@
         e = jnp.dot(own_t[r], far, preferred_element_type=f32)
         w = jnp.exp2(e)
         hi = w.astype(bf16)
-        lo = (w - hi.astype(f32)).astype(bf16)
         dims = (((1,), (1,)), ((), ()))
-        t = lax.dot_general(lhs, hi, dims, preferred_element_type=f32)
-        t = t + lax.dot_general(lhs, lo, dims, preferred_element_type=f32)
+        t = lax.dot_general(hi, lhs, dims, preferred_element_type=f32).T
         return t[0:8] + t[8:16] + t[16:24]
 
     per_row = fwd.shape[0] // rows
 
-    @pl.loop(0, rows)
+    @pl.loop(0, rows, unroll=2)
     def _(r):
         t = pairs(r, [fwd[r * per_row + k] for k in range(per_row)])
         acc[r] = t
 
-    unroll = 8
+    unroll = 16
 
     @pl.loop(0, rev_row.shape[0] // unroll)
     def _(g):

time: 263 us -> 175 us (0.67)
  Pallas kernels: 209 us -> 122 us
    pallas_call x2, Pallas kernels: 139 us -> 51.5 us  [contact_call(): pl.pallas_call(contact_kernel, out_shape=jax.ShapeDtypeStruct((rows, 8, w...]
  transfers between devices with their start and end apart: 8 -> 8, of which waited for: 3 -> 3; matrix products, arithmetic and copies ran while one was open for 1% -> 2% of each run, Pallas kernels for 40% -> 35%
where the time goes in v3:
time: 175 us
  Pallas kernels  122 us (70%)
  starting transfers between devices  22.8 us (13%)
  other arithmetic  12.7 us (7%)
  waiting for transfers between devices  9.66 us (6%)
  local copies, waits for them, and re-layouts  6.4 us (4%)
    pallas_call x2, Pallas kernels, gather_call(): pl.pallas_call(functools.partial(gather_kernel, count_gx, count_gy), out_...  70.3 us
    pallas_call x2, Pallas kernels, contact_call(): pl.pallas_call(contact_kernel, out_shape=jax.ShapeDtypeStruct((rows, 8, w...  51.5 us
    ppermute x4, starting transfers between devices, with_halo(): lax.ppermute(tail, axis, [(i, (i + 1) % count) for i in range(ends)])  13.5 us
    ppermute x4, starting transfers between devices, with_halo(): lax.ppermute(head, axis, [((i + 1) % count, i) for i in range(ends)])  9.27 us
    ppermute x4, waiting for transfers between devices, with_halo(): lax.ppermute(head, axis, [((i + 1) % count, i) for i in range(ends)])  6.99 us
  transfers between devices with their start and end apart: 8, of which 3 were waited for; matrix products, arithmetic and copies ran while one was open for 2% of the time, Pallas kernels for 35%

profile of v3, /device:TPU:9, one launch (start us, length us, event | category | flops | bytes accessed | tf_op | source)
XLA Modules:
  0.0 174.7 jit_solution(253342859316971888)
XLA Ops:
  0.8 1.0 select_bitcast_fusion
  1.7 0.9 pad_maximum_fusion.9
  2.6 3.2 %collective-permute-start = (f32[4,1,5,128]{3,1,2,0:T(1,128)S(1)}, f32[4,1,5,128]{3,1,2,0:T(1,128)S(1)}, u32[]{:S(2)}, u32[]{:S(2)}) collective-permute-start(f32[4,1,5,128]{3,1,2,0:T(1,128)S(1)} %get-tuple-element.62), channel_id=1, source_target_pairs={{0,8},{8,16},{16,24},{1,9},{9,17},{17,25},{2,10},{10,18},{18,26},{... | collective-permute-start | bytes 30728 | tf_op jit(solution)/shard_map/ppermute | solution.py:30
  5.8 2.1 %collective-permute-start.1 = (f32[4,1,5,128]{3,1,2,0:T(1,128)S(1)}, f32[4,1,5,128]{3,1,2,0:T(1,128)S(1)}, u32[]{:S(2)}, u32[]{:S(2)}) collective-permute-start(f32[4,1,5,128]{3,1,2,0:T(1,128)S(1)} %get-tuple-element.46), channel_id=1, source_target_pairs={{8,0},{16,8},{24,16},{9,1},{17,9},{25,17},{10,2},{18,10},{26,18},{... | collective-permute-start | bytes 30728 | tf_op jit(solution)/shard_map/ppermute | solution.py:32
  7.9 0.8 copy.32
  9.4 0.9 broadcast_multiply_fusion.1
  10.4 1.1 fusion.17
  11.6 4.9 %collective-permute-start.2 = (f32[4,34,5,1]{3,1,2,0:T(8,128)S(1)}, f32[4,34,5,1]{3,1,2,0:T(8,128)S(1)}, u32[]{:S(2)}, u32[]{:S(2)}) collective-permute-start(f32[4,34,5,1]{3,1,2,0:T(8,128)S(1)} %get-tuple-element.50), channel_id=1, source_target_pairs={{0,1},{1,2},{2,3},{3,4},{4,5},{5,6},{6,7},{8,9},{9,10},{10,11},{11... | collective-permute-start | bytes 8168 | tf_op jit(solution)/shard_map/ppermute | solution.py:30
  16.6 1.9 %collective-permute-start.3 = (f32[4,34,5,1]{3,1,2,0:T(8,128)S(1)}, f32[4,34,5,1]{3,1,2,0:T(8,128)S(1)}, u32[]{:S(2)}, u32[]{:S(2)}) collective-permute-start(f32[4,34,5,1]{3,1,2,0:T(8,128)S(1)} %get-tuple-element.51), channel_id=1, source_target_pairs={{1,0},{2,1},{3,2},{4,3},{5,4},{6,5},{7,6},{9,8},{10,9},{11,10},{12... | collective-permute-start | bytes 8168 | tf_op jit(solution)/shard_map/ppermute | solution.py:32
  18.8 2.7 %collective-permute-done.2 = f32[4,34,5,1]{3,1,2,0:T(8,128)S(1)} collective-permute-done((f32[4,34,5,1]{3,1,2,0:T(8,128)S(1)}, f32[4,34,5,1]{3,1,2,0:T(8,128)S(1)}, u32[]{:S(2)}, u32[]{:S(2)}) %collective-permute-start.2) | collective-permute-done | bytes 2752 | tf_op jit(solution)/shard_map/ppermute | solution.py:30
  21.4 6.0 %collective-permute-done.3 = f32[4,34,5,1]{3,1,2,0:T(8,128)S(1)} collective-permute-done((f32[4,34,5,1]{3,1,2,0:T(8,128)S(1)}, f32[4,34,5,1]{3,1,2,0:T(8,128)S(1)}, u32[]{:S(2)}, u32[]{:S(2)}) %collective-permute-start.3) | collective-permute-done | bytes 2752 | tf_op jit(solution)/shard_map/ppermute | solution.py:32
  31.1 34.6 %gather.2 = f32[32,264,128]{2,1,0:T(8,128)} custom-call(f32[264,128]{1,0:T(8,128)} %pad_maximum_fusion.7.own), custom_call_target="tpu_custom_call" | custom-call | tf_op jit(solution)/shard_map/gather/pallas_call | solution.py:208
  65.7 0.9 slice.227
  66.9 1.2 select_reduce_fusion
  69.5 25.7 %contact.2 = f32[32,8,128]{2,1,0:T(8,128)} custom-call(s32[256]{0:T(256)} %reshape.239.rev_row, s32[256]{0:T(256)} %reshape.240.rev_src, s32[256]{0:T(256)} %get-tuple-element.45.fwd, f32[256,128]{1,0:T(8,128)} %copy-done.1, f32[8448,128]{1,0:T(8,128)} %bitcast.77), custom_call_target="tpu_custom_call" | custom-call | tf_op jit(solution)/shard_map/contact/pallas_call | solution.py:119
  95.3 0.9 fusion.29
  96.8 1.9 %collective-permute-start.4 = (f32[4,1,5,128]{3,1,2,0:T(1,128)S(1)}, f32[4,1,5,128]{3,1,2,0:T(1,128)S(1)}, u32[]{:S(2)}, u32[]{:S(2)}) collective-permute-start(f32[4,1,5,128]{3,1,2,0:T(1,128)S(1)} %get-tuple-element.58), channel_id=1, source_target_pairs={{0,8},{8,16},{16,24},{1,9},{9,17},{17,25},{2,10},{10,18},{18,26},{... | collective-permute-start | bytes 30728 | tf_op jit(solution)/shard_map/ppermute | solution.py:30
  98.7 3.4 %collective-permute-start.5 = (f32[4,1,5,128]{3,1,2,0:T(1,128)S(1)}, f32[4,1,5,128]{3,1,2,0:T(1,128)S(1)}, u32[]{:S(2)}, u32[]{:S(2)}) collective-permute-start(f32[4,1,5,128]{3,1,2,0:T(1,128)S(1)} %get-tuple-element.59), channel_id=1, source_target_pairs={{8,0},{16,8},{24,16},{9,1},{17,9},{25,17},{10,2},{18,10},{26,18},{... | collective-permute-start | bytes 30728 | tf_op jit(solution)/shard_map/ppermute | solution.py:32
  102.2 0.9 collective-permute-done.5
  103.4 3.5 %collective-permute-start.6 = (f32[4,34,5,1]{3,1,2,0:T(8,128)S(1)}, f32[4,34,5,1]{3,1,2,0:T(8,128)S(1)}, u32[]{:S(2)}, u32[]{:S(2)}) collective-permute-start(f32[4,34,5,1]{3,1,2,0:T(8,128)S(1)} %get-tuple-element.48), channel_id=1, source_target_pairs={{0,1},{1,2},{2,3},{3,4},{4,5},{5,6},{6,7},{8,9},{9,10},{10,11},{11... | collective-permute-start | bytes 8168 | tf_op jit(solution)/shard_map/ppermute | solution.py:30
  106.9 1.9 %collective-permute-start.7 = (f32[4,34,5,1]{3,1,2,0:T(8,128)S(1)}, f32[4,34,5,1]{3,1,2,0:T(8,128)S(1)}, u32[]{:S(2)}, u32[]{:S(2)}) collective-permute-start(f32[4,34,5,1]{3,1,2,0:T(8,128)S(1)} %get-tuple-element.49), channel_id=1, source_target_pairs={{1,0},{2,1},{3,2},{4,3},{5,4},{6,5},{7,6},{9,8},{10,9},{11,10},{12... | collective-permute-start | bytes 8168 | tf_op jit(solution)/shard_map/ppermute | solution.py:32
  109.5 35.7 %gather.3 = f32[32,264,128]{2,1,0:T(8,128)} custom-call(f32[264,128]{1,0:T(8,128)} %pad_maximum_fusion.6.own), custom_call_target="tpu_custom_call" | custom-call | tf_op jit(solution)/shard_map/gather/pallas_call | solution.py:208
  145.2 25.8 %contact.3 = f32[32,8,128]{2,1,0:T(8,128)} custom-call(s32[256]{0:T(256)} %reshape.239.rev_row, s32[256]{0:T(256)} %reshape.240.rev_src, s32[256]{0:T(256)} %get-tuple-element.45.fwd, f32[256,128]{1,0:T(8,128)} %copy-done.2, f32[8448,128]{1,0:T(8,128)} %bitcast.78), custom_call_target="tpu_custom_call" | custom-call | tf_op jit(solution)/shard_map/contact/pallas_call | solution.py:119
  173.2 0.7 copy.37
  (78 shorter events, 10.9 us)
Async XLA Ops:
  2.6 7.7 %collective-permute-start = (f32[4,1,5,128]{3,1,2,0:T(1,128)S(1)}, f32[4,1,5,128]{3,1,2,0:T(1,128)S(1)}, u32[]{:S(2)}, u32[]{:S(2)}) collective-permute-start(f32[4,1,5,128]{3,1,2,0:T(1,128)S(1)} %get-tuple-element.62), channel_id=1, source_target_pairs={{0,8},{8,16},{16,24},{1,9},{9,17},{17,25},{2,10},{10,18},{18,26},{... | collective-permute-start | bytes 30728 | tf_op jit(solution)/shard_map/ppermute | solution.py:30
  5.8 4.5 %collective-permute-start.1 = (f32[4,1,5,128]{3,1,2,0:T(1,128)S(1)}, f32[4,1,5,128]{3,1,2,0:T(1,128)S(1)}, u32[]{:S(2)}, u32[]{:S(2)}) collective-permute-start(f32[4,1,5,128]{3,1,2,0:T(1,128)S(1)} %get-tuple-element.46), channel_id=1, source_target_pairs={{8,0},{16,8},{24,16},{9,1},{17,9},{25,17},{10,2},{18,10},{26,18},{... | collective-permute-start | bytes 30728 | tf_op jit(solution)/shard_map/ppermute | solution.py:32
  10.3 8.2 %copy-start.3 = (f32[3,32,5,128]{3,1,2,0:T(8,128)S(1)}, f32[3,32,5,128]{3,1,2,0:T(8,128)}, u32[]{:S(2)}) copy-start(f32[3,32,5,128]{3,1,2,0:T(8,128)} %param.10) | copy-start | bytes 737284
  11.4 16.0 %copy-start = (f32[3,32,5,128]{3,1,2,0:T(8,128)S(1)}, f32[3,32,5,128]{3,1,2,0:T(8,128)}, u32[]{:S(2)}) copy-start(f32[3,32,5,128]{3,1,2,0:T(8,128)} %param.9) | copy-start | bytes 737284
  11.6 9.8 %collective-permute-start.2 = (f32[4,34,5,1]{3,1,2,0:T(8,128)S(1)}, f32[4,34,5,1]{3,1,2,0:T(8,128)S(1)}, u32[]{:S(2)}, u32[]{:S(2)}) collective-permute-start(f32[4,34,5,1]{3,1,2,0:T(8,128)S(1)} %get-tuple-element.50), channel_id=1, source_target_pairs={{0,1},{1,2},{2,3},{3,4},{4,5},{5,6},{6,7},{8,9},{9,10},{10,11},{11... | collective-permute-start | bytes 8168 | tf_op jit(solution)/shard_map/ppermute | solution.py:30
  16.6 10.9 %collective-permute-start.3 = (f32[4,34,5,1]{3,1,2,0:T(8,128)S(1)}, f32[4,34,5,1]{3,1,2,0:T(8,128)S(1)}, u32[]{:S(2)}, u32[]{:S(2)}) collective-permute-start(f32[4,34,5,1]{3,1,2,0:T(8,128)S(1)} %get-tuple-element.51), channel_id=1, source_target_pairs={{1,0},{2,1},{3,2},{4,3},{5,4},{6,5},{7,6},{9,8},{10,9},{11,10},{12... | collective-permute-start | bytes 8168 | tf_op jit(solution)/shard_map/ppermute | solution.py:32
  30.4 35.3 %copy-start.1 = (f32[256,128]{1,0:T(8,128)}, f32[256,128]{1,0:T(8,128)S(1)}, u32[]{:S(2)}) copy-start(f32[256,128]{1,0:T(8,128)S(1)} %maximum_bitcast_fusion.own_ref) | copy-start | bytes 393220
  96.8 5.4 %collective-permute-start.4 = (f32[4,1,5,128]{3,1,2,0:T(1,128)S(1)}, f32[4,1,5,128]{3,1,2,0:T(1,128)S(1)}, u32[]{:S(2)}, u32[]{:S(2)}) collective-permute-start(f32[4,1,5,128]{3,1,2,0:T(1,128)S(1)} %get-tuple-element.58), channel_id=1, source_target_pairs={{0,8},{8,16},{16,24},{1,9},{9,17},{17,25},{2,10},{10,18},{18,26},{... | collective-permute-start | bytes 30728 | tf_op jit(solution)/shard_map/ppermute | solution.py:30
  98.7 4.4 %collective-permute-start.5 = (f32[4,1,5,128]{3,1,2,0:T(1,128)S(1)}, f32[4,1,5,128]{3,1,2,0:T(1,128)S(1)}, u32[]{:S(2)}, u32[]{:S(2)}) collective-permute-start(f32[4,1,5,128]{3,1,2,0:T(1,128)S(1)} %get-tuple-element.59), channel_id=1, source_target_pairs={{8,0},{16,8},{24,16},{9,1},{17,9},{25,17},{10,2},{18,10},{26,18},{... | collective-permute-start | bytes 30728 | tf_op jit(solution)/shard_map/ppermute | solution.py:32
  102.2 6.6 %copy-start.2 = (f32[256,128]{1,0:T(8,128)}, f32[256,128]{1,0:T(8,128)S(1)}, u32[]{:S(2)}) copy-start(f32[256,128]{1,0:T(8,128)S(1)} %maximum_bitcast_fusion.1.own_ref) | copy-start | bytes 393220
  103.4 67.5 %collective-permute-start.6 = (f32[4,34,5,1]{3,1,2,0:T(8,128)S(1)}, f32[4,34,5,1]{3,1,2,0:T(8,128)S(1)}, u32[]{:S(2)}, u32[]{:S(2)}) collective-permute-start(f32[4,34,5,1]{3,1,2,0:T(8,128)S(1)} %get-tuple-element.48), channel_id=1, source_target_pairs={{0,1},{1,2},{2,3},{3,4},{4,5},{5,6},{6,7},{8,9},{9,10},{10,11},{11... | collective-permute-start | bytes 8168 | tf_op jit(solution)/shard_map/ppermute | solution.py:30
  106.9 64.1 %collective-permute-start.7 = (f32[4,34,5,1]{3,1,2,0:T(8,128)S(1)}, f32[4,34,5,1]{3,1,2,0:T(8,128)S(1)}, u32[]{:S(2)}, u32[]{:S(2)}) collective-permute-start(f32[4,34,5,1]{3,1,2,0:T(8,128)S(1)} %get-tuple-element.49), channel_id=1, source_target_pairs={{1,0},{2,1},{3,2},{4,3},{5,4},{6,5},{7,6},{9,8},{10,9},{11,10},{12... | collective-permute-start | bytes 8168 | tf_op jit(solution)/shard_map/ppermute | solution.py:32
  172.1 0.9 copy-start.4

commit v4 on v3

--- a/solution.py
+++ b/solution.py
@@ -17,23 +17,6 @@
 
 bf16 = jnp.bfloat16
 f32 = jnp.float32
-
-
-def with_halo(cells, sides, width):
-    for axis, dim in sides:
-        count = lax.axis_size(axis)
-        ends = count - 1
-        head = lax.slice_in_dim(cells, 0, width, axis=dim)
-        tail = lax.slice_in_dim(cells, cells.shape[dim] - width, cells.shape[dim], axis=dim)
-        cells = jnp.concatenate(
-            [
-                lax.ppermute(tail, axis, [(i, (i + 1) % count) for i in range(ends)]),
-                cells,
-                lax.ppermute(head, axis, [((i + 1) % count, i) for i in range(ends)]),
-            ],
-            axis=dim,
-        )
-    return cells
 
 
 def internal_force(padded_disp, padded_stiff, displacement):
@@ -89,12 +72,12 @@
 
     per_row = fwd.shape[0] // rows
 
-    @pl.loop(0, rows, unroll=2)
+    @pl.loop(0, rows, unroll=4)
     def _(r):
         t = pairs(r, [fwd[r * per_row + k] for k in range(per_row)])
         acc[r] = t
 
-    unroll = 16
+    unroll = 32
 
     @pl.loop(0, rev_row.shape[0] // unroll)
     def _(g):
@@ -129,7 +112,20 @@
     )(rev_row, rev_src, fwd, own, everyone)
 
 
-def gather_kernel(count_gx, count_gy, own, out, local_sem, send_sems, recv_sems):
+def edge_pieces(columns):
+    tall = -(-columns // 8) * 8
+    pieces = []
+    start = 0
+    for dx in (-1, 0, 1):
+        for dy in (-1, 0, 1):
+            if (dx, dy) != (0, 0):
+                rows = tall if dy == 0 else 8
+                pieces.append((dx, dy, start, rows))
+                start += rows
+    return pieces, start
+
+
+def gather_kernel(count_gx, count_gy, pieces, own, edges, out, halo, local_sem, send_sems, recv_sems, edge_send, edge_recv):
     gx = lax.axis_index("gx")
     gy = lax.axis_index("gy")
     bits = count_gy.bit_length() - 1
@@ -141,10 +137,14 @@
 
     peers = [(lax.rem(gx + k, count_gx), gy) for k in range(1, count_gx)]
     peers += [(gx, gy + step) for step in steps]
+    around = [
+        (lax.rem(gx + dx + count_gx, count_gx), lax.rem(gy + dy + count_gy, count_gy))
+        for dx, dy, _, _ in pieces
+    ]
     barrier = pltpu.get_barrier_semaphore()
-    for peer in peers:
+    for peer in peers + around:
         pl.semaphore_signal(barrier, inc=1, device_id=peer, device_id_type=pl.DeviceIdType.MESH)
-    pl.semaphore_wait(barrier, len(peers))
+    pl.semaphore_wait(barrier, len(peers) + len(around))
 
     here = gx * count_gy + gy
     keep = pltpu.make_async_copy(own, out.at[here], local_sem)
@@ -175,6 +175,18 @@
 
     for peer in peers:
         send(None, peer)
+    edge_copies = []
+    for n, (dx, dy, start, rows) in enumerate(pieces):
+        copy = pltpu.make_async_remote_copy(
+            src_ref=edges.at[pl.ds(start, rows)],
+            dst_ref=halo.at[pl.ds(start, rows)],
+            send_sem=edge_send.at[n],
+            recv_sem=edge_recv.at[n],
+            device_id=around[n],
+            device_id_type=pl.DeviceIdType.MESH,
+        )
+        copy.start()
+        edge_copies.append(copy)
     half = 1 << (bits - 1)
     waves = [(k, m) for total in range(count_gx + half - 1) for m in range(half)
              for k in [total - m] if 0 <= k < count_gx and (k, m) != (0, 0)]
@@ -194,11 +206,13 @@
                 column = column + steps[bits - 2 - b]
         arrived(lax.rem(gx + k, count_gx) * count_gy + column)
     keep.wait()
+    for copy in edge_copies:
+        copy.wait()
     for copy in started:
         copy.wait_send()
 
 
-def gather_call(own, count_gx, count_gy):
+def gather_call(own, edges, pieces, count_gx, count_gy):
     devices_all = count_gx * count_gy
     bits = count_gy.bit_length() - 1
     half = count_gy // 2
@@ -206,18 +220,58 @@
     for m in range(half):
         sends += (count_gx - (m == 0)) * (bits - m.bit_length())
     return pl.pallas_call(
-        functools.partial(gather_kernel, count_gx, count_gy),
-        out_shape=jax.ShapeDtypeStruct((devices_all,) + own.shape, f32),
-        in_specs=[pl.BlockSpec(memory_space=pltpu.VMEM)],
-        out_specs=pl.BlockSpec(memory_space=pl.ANY),
+        functools.partial(gather_kernel, count_gx, count_gy, pieces),
+        out_shape=(
+            jax.ShapeDtypeStruct((devices_all,) + own.shape, f32),
+            jax.ShapeDtypeStruct(edges.shape, f32),
+        ),
+        in_specs=[pl.BlockSpec(memory_space=pltpu.VMEM)] * 2,
+        out_specs=(pl.BlockSpec(memory_space=pl.ANY), pl.BlockSpec(memory_space=pl.ANY)),
         scratch_shapes=[
             pltpu.SemaphoreType.DMA,
             pltpu.SemaphoreType.DMA((sends,)),
             pltpu.SemaphoreType.DMA((devices_all,)),
+            pltpu.SemaphoreType.DMA((len(pieces),)),
+            pltpu.SemaphoreType.DMA((len(pieces),)),
         ],
         compiler_params=pltpu.CompilerParams(collective_id=0, has_side_effects=True),
         name="gather",
-    )(own)
+    )(own, edges)
+
+
+def pack_edges(stacked, pieces):
+    fields, width_x, depth, width_y = stacked.shape
+    columns = fields * depth
+    sides_y = {-1: stacked[:, :, :, 0], 1: stacked[:, :, :, width_y - 1]}
+    parts = []
+    for dx, dy, _, rows in pieces:
+        x = 0 if dx < 0 else width_x - 1
+        if dy == 0:
+            part = stacked[:, x].reshape(columns, width_y)
+            part = jnp.pad(part, ((0, rows - columns), (0, 0)))
+        else:
+            part = sides_y[dy] if dx == 0 else sides_y[dy][:, x]
+            part = part.reshape(-1)
+            part = jnp.pad(part, (0, rows * width_y - part.shape[0])).reshape(rows, width_y)
+        parts.append(part)
+    return jnp.concatenate(parts, axis=0)
+
+
+def unpack_edges(halo, stacked, pieces):
+    fields, width_x, depth, width_y = stacked.shape
+    columns = fields * depth
+    got = {}
+    for dx, dy, start, rows in pieces:
+        part = halo[start : start + rows]
+        if dy == 0:
+            part = part[:columns].reshape(fields, 1, depth, width_y)
+        else:
+            tall = width_x if dx == 0 else 1
+            part = part.reshape(-1)[: columns * tall].reshape(fields, tall, depth, 1)
+        got[-dx, -dy] = part
+    got[0, 0] = stacked
+    lines = [jnp.concatenate([got[dx, dy] for dx in (-1, 0, 1)], axis=1) for dy in (-1, 0, 1)]
+    return jnp.concatenate(lines, axis=3)
 
 
 def local(displacement, velocity, stiffness, inverse_mass, facing):
@@ -249,6 +303,8 @@
     stiff_coef = penalty / (8.0 * width_y)
     damp_coef = damping / (8.0 * width_y)
 
+    pieces, _ = edge_pieces(4 * depth)
+
     for repeat in range(STEPS):
         p = displacement[:, :, depth - 1, :] + frame
         q = stiff_coef * p - damp_coef * velocity[:, :, depth - 1, :]
@@ -257,7 +313,11 @@
         surface = jnp.concatenate([sp, norm, jnp.ones_like(norm), q], axis=0).transpose(1, 0, 2)
         surface = surface.reshape(width_x * 8, width_y)
         tail = jnp.pad(fwd.astype(f32), (0, extra * 8 * width_y - requests)).reshape(extra * 8, width_y)
-        everyone = gather_call(jnp.concatenate([surface, tail], axis=0), count_gx, count_gy)
+        stacked = jnp.concatenate([displacement, masked_stiff[None]], axis=0)
+        edges = pack_edges(stacked, pieces)
+        everyone, halo = gather_call(
+            jnp.concatenate([surface, tail], axis=0), edges, pieces, count_gx, count_gy
+        )
         if repeat == 0:
             table = everyone[:, width_x * 8 :].reshape(devices_all, -1)[:, :requests].astype(jnp.int32)
             mine = table // unit == me
@@ -270,8 +330,7 @@
             source = jnp.arange(devices_all, dtype=jnp.int32)[:, None] * unit + (ordinal // per_row)[None, :]
             rev_src = jnp.sum(jnp.where(pick, source[:, None, :], 0), axis=2).reshape(requests)
         everyone = everyone.reshape(-1, width_y)
-        stacked = jnp.concatenate([displacement, masked_stiff[None]], axis=0)
-        padded = with_halo(stacked, (("gx", 1), ("gy", 3)), 1)
+        padded = unpack_edges(halo, stacked, pieces)
         padded = jnp.pad(padded, ((0, 0), (0, 0), (1, 1), (0, 0)))
         internal = internal_force(padded[:3], padded[3], displacement)
         contact = contact_call(rev_row, rev_src, fwd, surface, everyone)

time: 175 us -> 156 us (0.89)
  starting transfers between devices: 22.8 us -> 0 us
  local copies, waits for them, and re-layouts: 6.4 us -> 24 us
  waiting for transfers between devices: 9.66 us -> 0 us
  Pallas kernels: 122 us -> 115 us
  other arithmetic: 12.7 us -> 15 us
    ppermute x8 -> x0, starting transfers between devices: 22.8 us -> none  [the longest x4 13.5 us: with_halo(): lax.ppermute(tail, axis, [(i, (i + 1) % count) for i in range(ends)])]
    pallas_call x2, Pallas kernels: 51.5 us -> 41.3 us  [contact_call(): pl.pallas_call(contact_kernel, out_shape=jax.ShapeDtypeStruct((rows, 8, w...]
    ppermute x8 -> x0, waiting for transfers between devices: 9.66 us -> none  [the longest x4 6.99 us: with_halo(): lax.ppermute(head, axis, [((i + 1) % count, i) for i in range(ends)])]
    slice x2 -> x37, local copies, waits for them, and re-layouts: 0.37 us -> 8.04 us  [the longest x8 4.23 us: pack_edges(): sides_y = {-1: stacked[:, :, :, 0], 1: stacked[:, :, :, width_y - 1]}]
    reshape x0 -> x28, local copies, waits for them, and re-layouts: none -> 6.92 us  [the longest x22 6.87 us: unpack_edges(): part = part.reshape(-1)[:columns * tall].reshape(fields, tall, depth, 1)]
    pallas_call x2, Pallas kernels: 70.3 us -> 73.2 us  [gather_call(): pl.pallas_call(functools.partial(gather_kernel, count_gx, count_gy, piece...]
    unnamed x15 -> x34, local copies, waits for them, and re-layouts: 2.88 us -> 4.67 us
  transfers between devices with their start and end apart: 8 -> 0, of which waited for: 3 -> 0; matrix products, arithmetic and copies ran while one was open for 2% -> 0% of each run, Pallas kernels for 35% -> 0%
where the time goes in v4:
time: 156 us; the launch traced here: 155 us
  Pallas kernels  115 us (74%)
  local copies, waits for them, and re-layouts  24 us (15%)
  other arithmetic  15 us (10%)
    pallas_call x2, Pallas kernels, gather_call(): pl.pallas_call(functools.partial(gather_kernel, count_gx, count_gy, piece...  73.2 us
    pallas_call x2, Pallas kernels, contact_call(): pl.pallas_call(contact_kernel, out_shape=jax.ShapeDtypeStruct((rows, 8, w...  41.3 us
    reshape x22, local copies, waits for them, and re-layouts, unpack_edges(): part = part.reshape(-1)[:columns * tall].reshape(fields, tall, depth, 1)  6.87 us
    unnamed x34, local copies, waits for them, and re-layouts  4.67 us
    slice x8, local copies, waits for them, and re-layouts, pack_edges(): sides_y = {-1: stacked[:, :, :, 0], 1: stacked[:, :, :, width_y - 1]}  4.23 us

profile of v4, /device:TPU:9, one launch (start us, length us, event | category | flops | bytes accessed | tf_op | source)
XLA Modules:
  0.0 155.1 jit_solution(12594852482982526990)
XLA Ops:
  0.9 0.8 copy.141
  2.3 1.0 fusion.52
  3.3 0.9 fusion.33
  4.3 1.0 and_select_fusion
  5.2 0.9 broadcast_multiply_fusion.2
  6.1 0.8 multiply_reduce_fusion.1
  8.2 0.9 copy.147
  9.5 0.9 copy.146
  12.2 38.0 %gather.2 = (f32[32,264,128]{2,1,0:T(8,128)}, f32[96,128]{1,0:T(8,128)}) custom-call(f32[264,128]{1,0:T(8,128)} %pad_maximum_fusion.3.own, f32[96,128]{1,0:T(8,128)} %copy-done.5), custom_call_target="tpu_custom_call" | custom-call | tf_op jit(solution)/shard_map/gather/pallas_call | solution.py:222
  51.6 0.7 fusion.46
  53.2 0.9 slice.359
  54.4 1.2 select_reduce_fusion
  57.0 20.8 %contact.2 = f32[32,8,128]{2,1,0:T(8,128)} custom-call(s32[256]{0:T(256)} %reshape.377.rev_row, s32[256]{0:T(256)} %reshape.378.rev_src, s32[256]{0:T(256)} %get-tuple-element.57.fwd, f32[256,128]{1,0:T(8,128)} %bitcast.177, f32[8448,128]{1,0:T(8,128)} %bitcast.171), custom_call_target="tpu_custom_call" | custom-call | tf_op jit(solution)/shard_map/contact/pallas_call | solution.py:102
  77.8 0.9 slice.430
  78.7 1.0 copy.154
  79.7 1.0 copy.151
  84.9 0.9 copy.169
  86.2 0.9 copy.168
  89.0 35.2 %gather.3 = (f32[32,264,128]{2,1,0:T(8,128)}, f32[96,128]{1,0:T(8,128)}) custom-call(f32[264,128]{1,0:T(8,128)} %pad_maximum_fusion.2.own, f32[96,128]{1,0:T(8,128)} %copy-done.6), custom_call_target="tpu_custom_call" | custom-call | tf_op jit(solution)/shard_map/gather/pallas_call | solution.py:222
  124.2 20.6 %contact.3 = f32[32,8,128]{2,1,0:T(8,128)} custom-call(s32[256]{0:T(256)} %reshape.377.rev_row, s32[256]{0:T(256)} %reshape.378.rev_src, s32[256]{0:T(256)} %get-tuple-element.57.fwd, f32[256,128]{1,0:T(8,128)} %bitcast.179, f32[8448,128]{1,0:T(8,128)} %bitcast.172), custom_call_target="tpu_custom_call" | custom-call | tf_op jit(solution)/shard_map/contact/pallas_call | solution.py:102
  146.1 1.1 copy.179
  147.2 1.1 copy.174
  148.3 2.2 %fusion.3 = f32[4,34,7,130]{3,0,1,2:T(4,128)S(1)} fusion(f32[4,1,5,1]{3,0,1,2:T(4,128)S(1)} %copy.180, f32[4,32,5,1]{3,0,1,2:T(4,128)S(1)} %copy.179, f32[4,1,5,1]{3,0,1,2:T(4,128)S(1)} %copy.178, f32[4,1,5,128]{3,0,1,2:T(4,128)S(1)} %copy.177, f32[4,1,5,1]{3,0,1,2:T(4,128)S(1)} %copy.175, f32[4,1,5,128]{3,0,1,2:T(4,128)S(1)} %copy.176, ...), kind=kLoop, calls=%fused_computation.17 | loop fusion | flops 2722720 | bytes 848640 | tf_op jit(solution)/shard_map/concatenate | solution.py:274
  153.7 0.7 copy.186
  (163 shorter events, 19.3 us)
Async XLA Ops:
  0.6 7.2 %copy-start = (f32[3,32,5,128]{3,1,2,0:T(8,128)S(1)}, f32[3,32,5,128]{3,1,2,0:T(8,128)}, u32[]{:S(2)}) copy-start(f32[3,32,5,128]{3,1,2,0:T(8,128)} %param.9) | copy-start | bytes 737284
  7.2 2.3 %copy-start.1 = (f32[32,8,128]{2,1,0:T(8,128)}, f32[32,8,128]{2,1,0:T(8,128)S(1)}, u32[]{:S(2)}) copy-start(f32[32,8,128]{2,1,0:T(8,128)S(1)} %copy.219) | copy-start | bytes 393220
  11.6 0.6 copy-start.5
  82.0 0.9 copy-start.3
  83.6 2.6 %copy-start.2 = (f32[32,8,128]{2,1,0:T(8,128)}, f32[32,8,128]{2,1,0:T(8,128)S(1)}, u32[]{:S(2)}) copy-start(f32[32,8,128]{2,1,0:T(8,128)S(1)} %copy.218) | copy-start | bytes 393220
  88.4 0.6 copy-start.6
  124.2 20.6 %copy-start.7 = (f32[96,128]{1,0:T(8,128)S(1)}, f32[96,128]{1,0:T(8,128)}, u32[]{:S(2)}) copy-start(f32[96,128]{1,0:T(8,128)} %get-tuple-element.32) | copy-start | bytes 147460
  152.4 0.9 copy-start.4

commit v5 on v4

--- a/solution.py
+++ b/solution.py
@@ -72,7 +72,7 @@
 
     per_row = fwd.shape[0] // rows
 
-    @pl.loop(0, rows, unroll=4)
+    @pl.loop(0, rows, unroll=8)
     def _(r):
         t = pairs(r, [fwd[r * per_row + k] for k in range(per_row)])
         acc[r] = t

time: 156 us -> 153 us (0.981)
  Pallas kernels: 115 us -> 112 us
    pallas_call x2, Pallas kernels: 41.3 us -> 38.6 us  [contact_call(): pl.pallas_call(contact_kernel, out_shape=jax.ShapeDtypeStruct((rows, 8, w...]
where the time goes in v5:
time: 153 us; the launch traced here: 152 us
  Pallas kernels  112 us (73%)
  local copies, waits for them, and re-layouts  24 us (16%)
  other arithmetic  15 us (10%)
    pallas_call x2, Pallas kernels, gather_call(): pl.pallas_call(functools.partial(gather_kernel, count_gx, count_gy, piece...  73.2 us
    pallas_call x2, Pallas kernels, contact_call(): pl.pallas_call(contact_kernel, out_shape=jax.ShapeDtypeStruct((rows, 8, w...  38.6 us
    reshape x22, local copies, waits for them, and re-layouts, unpack_edges(): part = part.reshape(-1)[:columns * tall].reshape(fields, tall, depth, 1)  6.87 us
    unnamed x34, local copies, waits for them, and re-layouts  4.67 us
    slice x8, local copies, waits for them, and re-layouts, pack_edges(): sides_y = {-1: stacked[:, :, :, 0], 1: stacked[:, :, :, width_y - 1]}  4.23 us

profile of v5, /device:TPU:9, one launch (start us, length us, event | category | flops | bytes accessed | tf_op | source)
XLA Modules:
  0.0 152.4 jit_solution(7830254722988014210)
XLA Ops:
  0.9 0.8 copy.141
  2.3 1.0 fusion.52
  3.3 0.9 fusion.33
  4.3 1.0 and_select_fusion
  5.2 0.9 broadcast_multiply_fusion.2
  6.1 0.8 multiply_reduce_fusion.1
  8.2 0.9 copy.147
  9.5 0.9 copy.146
  12.2 38.0 %gather.2 = (f32[32,264,128]{2,1,0:T(8,128)}, f32[96,128]{1,0:T(8,128)}) custom-call(f32[264,128]{1,0:T(8,128)} %pad_maximum_fusion.3.own, f32[96,128]{1,0:T(8,128)} %copy-done.5), custom_call_target="tpu_custom_call" | custom-call | tf_op jit(solution)/shard_map/gather/pallas_call | solution.py:222
  51.6 0.7 fusion.46
  53.2 0.9 slice.359
  54.4 1.2 select_reduce_fusion
  57.0 19.4 %contact.2 = f32[32,8,128]{2,1,0:T(8,128)} custom-call(s32[256]{0:T(256)} %reshape.377.rev_row, s32[256]{0:T(256)} %reshape.378.rev_src, s32[256]{0:T(256)} %get-tuple-element.57.fwd, f32[256,128]{1,0:T(8,128)} %bitcast.177, f32[8448,128]{1,0:T(8,128)} %bitcast.171), custom_call_target="tpu_custom_call" | custom-call | tf_op jit(solution)/shard_map/contact/pallas_call | solution.py:102
  76.4 0.9 slice.430
  77.3 1.0 copy.154
  78.3 1.0 copy.151
  83.6 0.9 copy.169
  84.8 0.9 copy.168
  87.6 35.3 %gather.3 = (f32[32,264,128]{2,1,0:T(8,128)}, f32[96,128]{1,0:T(8,128)}) custom-call(f32[264,128]{1,0:T(8,128)} %pad_maximum_fusion.2.own, f32[96,128]{1,0:T(8,128)} %copy-done.6), custom_call_target="tpu_custom_call" | custom-call | tf_op jit(solution)/shard_map/gather/pallas_call | solution.py:222
  122.9 19.2 %contact.3 = f32[32,8,128]{2,1,0:T(8,128)} custom-call(s32[256]{0:T(256)} %reshape.377.rev_row, s32[256]{0:T(256)} %reshape.378.rev_src, s32[256]{0:T(256)} %get-tuple-element.57.fwd, f32[256,128]{1,0:T(8,128)} %bitcast.179, f32[8448,128]{1,0:T(8,128)} %bitcast.172), custom_call_target="tpu_custom_call" | custom-call | tf_op jit(solution)/shard_map/contact/pallas_call | solution.py:102
  143.3 1.1 copy.179
  144.4 1.1 copy.174
  145.5 2.2 %fusion.3 = f32[4,34,7,130]{3,0,1,2:T(4,128)S(1)} fusion(f32[4,1,5,1]{3,0,1,2:T(4,128)S(1)} %copy.180, f32[4,32,5,1]{3,0,1,2:T(4,128)S(1)} %copy.179, f32[4,1,5,1]{3,0,1,2:T(4,128)S(1)} %copy.178, f32[4,1,5,128]{3,0,1,2:T(4,128)S(1)} %copy.177, f32[4,1,5,1]{3,0,1,2:T(4,128)S(1)} %copy.175, f32[4,1,5,128]{3,0,1,2:T(4,128)S(1)} %copy.176, ...), kind=kLoop, calls=%fused_computation.17 | loop fusion | flops 2722720 | bytes 848640 | tf_op jit(solution)/shard_map/concatenate | solution.py:274
  151.0 0.7 copy.186
  (163 shorter events, 19.3 us)
Async XLA Ops:
  0.6 7.2 %copy-start = (f32[3,32,5,128]{3,1,2,0:T(8,128)S(1)}, f32[3,32,5,128]{3,1,2,0:T(8,128)}, u32[]{:S(2)}) copy-start(f32[3,32,5,128]{3,1,2,0:T(8,128)} %param.9) | copy-start | bytes 737284
  7.2 2.3 %copy-start.1 = (f32[32,8,128]{2,1,0:T(8,128)}, f32[32,8,128]{2,1,0:T(8,128)S(1)}, u32[]{:S(2)}) copy-start(f32[32,8,128]{2,1,0:T(8,128)S(1)} %copy.219) | copy-start | bytes 393220
  11.6 0.6 copy-start.5
  80.6 0.9 copy-start.3
  82.2 2.6 %copy-start.2 = (f32[32,8,128]{2,1,0:T(8,128)}, f32[32,8,128]{2,1,0:T(8,128)S(1)}, u32[]{:S(2)}) copy-start(f32[32,8,128]{2,1,0:T(8,128)S(1)} %copy.218) | copy-start | bytes 393220
  87.0 0.6 copy-start.6
  122.9 19.2 %copy-start.7 = (f32[96,128]{1,0:T(8,128)S(1)}, f32[96,128]{1,0:T(8,128)}, u32[]{:S(2)}) copy-start(f32[96,128]{1,0:T(8,128)} %get-tuple-element.32) | copy-start | bytes 147460
  149.7 0.9 copy-start.4
